TPU v7x, 32 devices: a whole 2x2x4 slice. The times are simulated.
32 devices in a mesh: dp: 4 (over y, core), seq: 8 (over z, x).
Axes of the slice: x: 2, y: 2, z: 4, core: 2. Of those that a mesh axis runs over, the one named last changes fastest.
Arguments:
- queries: bfloat16 [12288, 14, 128], P(('dp', 'seq')), parts along dimension 0, may hold values from -24 to 24
- key_heads: bfloat16 [12288, 2, 128], P(('dp', 'seq')), parts along dimension 0, may hold values from -24 to 24
- value_heads: bfloat16 [12288, 2, 128], P(('dp', 'seq')), parts along dimension 0, may hold values from -6 to 6
- output_grad: bfloat16 [12288, 14, 128], P(('dp', 'seq')), parts along dimension 0, may hold values from -24 to 24
- window: int32 [96], P(('dp', 'seq')), parts along dimension 0, may hold values from 1 to 4
- retrieved: int32 [96, 4], P(('dp', 'seq')), parts along dimension 0, may hold values from 0 to 21, as said below
Outputs:
- query_grad: bfloat16 [12288, 14, 128], P(('dp', 'seq')), parts along dimension 0
- key_grad: bfloat16 [12288, 2, 128], P(('dp', 'seq')), parts along dimension 0
- value_grad: bfloat16 [12288, 2, 128], P(('dp', 'seq')), parts along dimension 0
There are 4 independent parts, one for each index of `dp`. A program takes and returns all parts, laid end to end along the dimension named above; each array names one. Nothing has to cross between parts.
Inputs may be any that keep to these rules, and one draw needn't show every extreme that they name: retrieved[i, r] is at most i. The entries of the 3 query blocks g * 3 to g * 3 + 2 name at most one distinct block among the blocks d * 3 to d * 3 + 2, for every g and d.
All inputs are finite; a program needn't handle non-finite values.
Results may differ from a plain program's by a relative error of at most 0.0075.
Values may be sent and summed in bfloat16 or wider, within the bound.
No kernel may reach another device: no remote copies, remote signals or barrier semaphores. Data moves between devices by JAX's collectives and lax.ppermute only.
A program may use at most 128 MiB of HBM per device.

v0:
```python
import jax
import jax.numpy as jnp
from jax import lax
from jax.sharding import PartitionSpec as P

HD = 128
QH = 14
KVH = 2
BLOCK = 128
MEMORY = 4


masked_score = -1e30


def shifted(array, axis, by):
    length = lax.axis_size(axis)
    pairs = [(i, i + by) for i in range(length) if 0 <= i + by < length]
    return lax.ppermute(array, axis, pairs)


def attend(query_block, grad_block, key_rows, value_rows, allowed, score_scale):
    scores = (
        jnp.einsum("qhgd,khd->hgqk", query_block, key_rows, preferred_element_type=jnp.float32)
        * score_scale
    )
    scores = jnp.where(allowed[None, None], scores, masked_score)
    row_max = jnp.max(scores, axis=-1, keepdims=True)
    weights = jnp.where(allowed[None, None], jnp.exp(scores - row_max), 0.0)
    row_total = jnp.sum(weights, axis=-1, keepdims=True)
    probs = weights / row_total
    probs_half = probs.astype(jnp.bfloat16)
    outputs = jnp.einsum(
        "hgqk,khd->qhgd", probs_half, value_rows, preferred_element_type=jnp.float32
    )
    delta = jnp.moveaxis(jnp.sum(grad_block.astype(jnp.float32) * outputs, axis=-1), 0, -1)
    grad_probs = jnp.einsum(
        "qhgd,khd->hgqk", grad_block, value_rows, preferred_element_type=jnp.float32
    )
    grad_scores = (probs * (grad_probs - delta[..., None])).astype(jnp.bfloat16)
    query_grad = (
        jnp.einsum("hgqk,khd->qhgd", grad_scores, key_rows, preferred_element_type=jnp.float32)
        * score_scale
    )
    key_grad = (
        jnp.einsum("hgqk,qhgd->khd", grad_scores, query_block, preferred_element_type=jnp.float32)
        * score_scale
    )
    value_grad = jnp.einsum(
        "hgqk,qhgd->khd", probs_half, grad_block, preferred_element_type=jnp.float32
    )
    return (query_grad, key_grad, value_grad)


def body(queries, key_heads, value_heads, output_grad, window, retrieved):
    tokens = queries.shape[0]
    per_device = tokens // BLOCK
    near_count = per_device + 1
    cand_count = near_count + MEMORY
    group_size = QH // KVH
    score_scale = HD ** (-0.5)
    shards = lax.axis_size("seq")
    own_index = lax.axis_index("seq")
    key_value = jnp.stack([key_heads, value_heads]).reshape(2, per_device, BLOCK, KVH, HD)
    earlier = shifted(key_value, "seq", 1)
    joined = jnp.concatenate([earlier, key_value], axis=1)
    query_blocks = queries.reshape(per_device, BLOCK, KVH, group_size, HD)
    grad_blocks = output_grad.reshape(per_device, BLOCK, KVH, group_size, HD)
    first_block = own_index * per_device
    near_offsets = jnp.arange(near_count, dtype=jnp.int32)
    key_index = jnp.arange(cand_count * BLOCK, dtype=jnp.int32)
    query_index = jnp.arange(BLOCK, dtype=jnp.int32)
    causal = (key_index[None, :] // BLOCK != near_count - 1) | (
        key_index[None, :] % BLOCK <= query_index[:, None]
    )
    earlier_entry = jnp.arange(MEMORY)[None, :] < jnp.arange(MEMORY)[:, None]

    def block_masks(index):
        block_row = first_block + index
        earliest = block_row - window[index]
        near_blocks = block_row - per_device + near_offsets
        near_live = (near_blocks >= 0) & (near_blocks > earliest)
        memory_rows = retrieved[index]
        repeated = jnp.any((memory_rows[:, None] == memory_rows[None, :]) & earlier_entry, axis=1)
        far_live = (memory_rows <= earliest) & jnp.logical_not(repeated)
        block_live = jnp.concatenate([near_live, far_live])
        return (jnp.repeat(block_live, BLOCK)[None, :] & causal, memory_rows)

    all_lists = lax.all_gather(retrieved, "seq", axis=0, tiled=True)
    wanted = jnp.where(all_lists // per_device == own_index, all_lists % per_device, -1)
    wanted = jnp.max(wanted.reshape(shards, per_device * MEMORY), axis=1)
    outgoing = jnp.take(key_value, jnp.maximum(wanted, 0), axis=1)
    arrived = lax.all_to_all(outgoing, "seq", split_axis=1, concat_axis=1, tiled=True)

    def fetch_memory(memory_rows):
        return jnp.take(arrived, memory_rows // per_device, axis=1)

    def block_step(near_sum, index):
        allowed, memory_rows = block_masks(index)
        near_pair = lax.dynamic_slice_in_dim(joined, index, near_count, axis=1)
        candidates = jnp.concatenate([near_pair, fetch_memory(memory_rows)], axis=1)
        candidates = candidates.reshape(2, cand_count * BLOCK, KVH, HD)
        query_grad, key_grad, value_grad = attend(
            query_blocks[index],
            grad_blocks[index],
            candidates[0],
            candidates[1],
            allowed,
            score_scale,
        )
        grads = jnp.stack([key_grad, value_grad]).reshape(2, cand_count, BLOCK, KVH, HD)
        current = lax.dynamic_slice_in_dim(near_sum, index, near_count, axis=1)
        near_sum = lax.dynamic_update_slice_in_dim(
            near_sum, current + grads[:, :near_count], index, axis=1
        )
        far_grads = jnp.moveaxis(grads[:, near_count:], 1, 0)
        return (near_sum, (query_grad.reshape(BLOCK, QH, HD).astype(jnp.bfloat16), far_grads))

    near_zero = jnp.zeros((2, 2 * per_device, BLOCK, KVH, HD), jnp.float32)
    near_sum, (query_grads, far_grads) = lax.scan(
        block_step, near_zero, jnp.arange(per_device, dtype=jnp.int32)
    )
    entries = far_grads.reshape(per_device * MEMORY, 2, BLOCK, KVH, HD)
    entry_rows = retrieved.reshape(per_device * MEMORY)
    owner_hits = (entry_rows[:, None] // per_device == jnp.arange(shards)[None, :]).astype(
        jnp.float32
    )
    by_owner = jnp.einsum("ne,nxbhd->exbhd", owner_hits, entries, precision=lax.Precision.HIGHEST)
    replies = lax.all_to_all(
        by_owner.astype(jnp.bfloat16), "seq", split_axis=0, concat_axis=0, tiled=True
    )
    slot_hits = (wanted[:, None] == jnp.arange(per_device)[None, :]).astype(jnp.bfloat16)
    far_sum = jnp.einsum("eb,exchd->xbchd", slot_hits, replies, preferred_element_type=jnp.float32)
    returned = shifted(near_sum[:, :per_device].astype(jnp.bfloat16), "seq", -1).astype(jnp.float32)
    summed = near_sum[:, per_device:] + returned + far_sum
    key_grad = summed[0].reshape(tokens, KVH, HD).astype(jnp.bfloat16)
    value_grad = summed[1].reshape(tokens, KVH, HD).astype(jnp.bfloat16)
    return (query_grads.reshape(tokens, QH, HD), key_grad, value_grad)


def solution(mesh):
    placed = (
        P(("dp", "seq"), None, None),
        P(("dp", "seq"), None, None),
        P(("dp", "seq"), None, None),
        P(("dp", "seq"), None, None),
        P(("dp", "seq")),
        P(("dp", "seq"), None),
    )
    return jax.shard_map(
        body,
        mesh=mesh,
        in_specs=placed,
        out_specs=(
            P(("dp", "seq"), None, None),
            P(("dp", "seq"), None, None),
            P(("dp", "seq"), None, None),
        ),
        check_vma=False,
    )
```

profile of v0, /device:TPU:14, one launch (start us, length us, event | category | flops | bytes accessed | tf_op | source)
XLA Modules:
  0.0 238.7 jit_solution(1864630172533657820)
XLA Ops:
  0.6 25.2 %all-gather = s32[8,3,4]{2,1,0:T(4,128)S(1)} all-gather(s32[1,3,4]{2,1,0:T(4,128)} %bitcast.238), channel_id=1, replica_groups=mesh['dp'=4,'seq'=8] {'seq'}, dimensions={0}, use_global_device_ids=true | all-gather | bytes 432 | tf_op jit(solution)/shard_map/all_gather | solution.py:89
  31.1 5.7 %all-to-all-start = ((bf16[2,8,128,2,128]{4,2,3,0,1:T(8,128)(2,1)}), bf16[2,8,128,2,128]{4,2,3,0,1:T(8,128)(2,1)S(1)}, u32[]{:S(2)}, u32[]{:S(2)}) async-start(bf16[2,8,128,2,128]{4,2,3,0,1:T(8,128)(2,1)} %select_bitcast_fusion), calls=%async_computation | async-start | bytes 2097152 | tf_op jit(solution)/shard_map/all_to_all | solution.py:93
  36.8 3.4 %collective-permute-start = (bf16[2,3,128,2,128]{4,2,3,1,0:T(8,128)(2,1)S(1)}, bf16[2,3,128,2,128]{4,2,3,1,0:T(8,128)(2,1)S(1)}, u32[]{:S(2)}, u32[]{:S(2)}) collective-permute-start(bf16[2,3,128,2,128]{4,2,3,1,0:T(8,128)(2,1)S(1)} %copy_dynamic-update-slice_fusion), channel_id=1, source_target_pairs={{0,1},{1,2},{2,3},{3,4},{4,5},{5,6},{6,7},{8,9},{9,10},{10,11},{11... | collective-permute-start | bytes 1179656 | tf_op jit(solution)/shard_map/ppermute | solution.py:19
  41.0 22.6 %collective-permute-done = bf16[2,3,128,2,128]{4,2,3,1,0:T(8,128)(2,1)S(1)} collective-permute-done((bf16[2,3,128,2,128]{4,2,3,1,0:T(8,128)(2,1)S(1)}, bf16[2,3,128,2,128]{4,2,3,1,0:T(8,128)(2,1)S(1)}, u32[]{:S(2)}, u32[]{:S(2)}) %collective-permute-start) | collective-permute-done | bytes 393248 | tf_op jit(solution)/shard_map/ppermute | solution.py:19
  64.7 2.1 copy.180
  68.1 123.7 %while.17 = (s32[]{:T(128)}, f32[2,6,128,2,128]{4,2,3,1,0:T(8,128)}, bf16[3,128,14,128]{3,1,0,2:T(8,128)(2,1)}, f32[3,4,2,128,2,128]{5,3,4,2,1,0:T(8,128)}, s32[...) while((s32[]{:T(128)}, ...), condition=%wide.region_7.8_spmd.clone, body=%wide.region_2.7_spmd.clone.sunk | while | flops 2841608704 | bytes 122208880 | solution.py:120
  74.5 2.8 %gather_fusion = bf16[4,2,128,2,128]{4,3,2,1,0:T(2,128)(2,1)S(1)} fusion(bf16[2,8,128,2,128]{4,3,2,1,0:T(2,128)(2,1)} %get-tuple-element.506, s32[1024]{0:T(1024)S(1)} %pad_clamp_fusion.3), kind=kCustom, calls=%fused_computation.clone.clone.1 | custom fusion | bytes 1048592 | tf_op jit(solution)/shard_map/while/body/eval_jaxpr/jit(_take)/gather | solution.py:96
  77.9 2.1 copy.246
  82.4 6.8 %fusion.138 = (f32[2,7,128]{2,1,0:T(8,128)S(1)}, f32[2,7,128,1024]{2,3,1,0:T(8,128)}) fusion(pred[128,1024]{0,1:T(8,128)(4,1)S(1)} %fusion.137, bf16[1024,2,128,1]{2,0,3,1:T(8,128)(2,1)S(1)} %bitcast.225, bf16[3,128,2,7,128]{4,1,0,3,2:T(8,128)(2,1)} %get-tuple-element.501, s32[]{:T(128)S(6)} %select_n.212), kind=kOutput, calls=%fused_computation.125.clone.1 | convolution fusion | flops 478938112 | bytes 8592388 | tf_op jit(solution)/shard_map/while/body/eval_jaxpr/sub | solution.py:29
  89.3 4.1 %fusion.139 = bf16[2,7,128,1024]{2,3,1,0:T(8,128)(2,1)S(1)} fusion(f32[2,7,128,1024]{2,3,1,0:T(8,128)} %get-tuple-element.454, f32[2,7,128]{2,1,0:T(8,128)S(1)} %get-tuple-element.455), kind=kLoop, calls=%fused_computation.16.clone.1 | loop fusion | flops 3670016 | bytes 11017216 | tf_op jit(solution)/shard_map/while/body/eval_jaxpr/convert_element_type | solution.py:32
  99.4 2.4 fusion.142
  115.7 2.8 %gather_fusion = bf16[4,2,128,2,128]{4,3,2,1,0:T(2,128)(2,1)S(1)} fusion(bf16[2,8,128,2,128]{4,3,2,1,0:T(2,128)(2,1)} %get-tuple-element.506, s32[1024]{0:T(1024)S(1)} %pad_clamp_fusion.3), kind=kCustom, calls=%fused_computation.clone.clone.1 | custom fusion | bytes 1048592 | tf_op jit(solution)/shard_map/while/body/eval_jaxpr/jit(_take)/gather | solution.py:96
  123.7 6.8 %fusion.138 = (f32[2,7,128]{2,1,0:T(8,128)S(1)}, f32[2,7,128,1024]{2,3,1,0:T(8,128)}) fusion(pred[128,1024]{0,1:T(8,128)(4,1)S(1)} %fusion.137, bf16[1024,2,128,1]{2,0,3,1:T(8,128)(2,1)S(1)} %bitcast.225, bf16[3,128,2,7,128]{4,1,0,3,2:T(8,128)(2,1)} %get-tuple-element.501, s32[]{:T(128)S(6)} %select_n.212), kind=kOutput, calls=%fused_computation.125.clone.1 | convolution fusion | flops 478938112 | bytes 8592388 | tf_op jit(solution)/shard_map/while/body/eval_jaxpr/sub | solution.py:29
  130.5 4.1 %fusion.139 = bf16[2,7,128,1024]{2,3,1,0:T(8,128)(2,1)S(1)} fusion(f32[2,7,128,1024]{2,3,1,0:T(8,128)} %get-tuple-element.454, f32[2,7,128]{2,1,0:T(8,128)S(1)} %get-tuple-element.455), kind=kLoop, calls=%fused_computation.16.clone.1 | loop fusion | flops 3670016 | bytes 11017216 | tf_op jit(solution)/shard_map/while/body/eval_jaxpr/convert_element_type | solution.py:32
  140.6 2.4 fusion.142
  157.0 2.8 %gather_fusion = bf16[4,2,128,2,128]{4,3,2,1,0:T(2,128)(2,1)S(1)} fusion(bf16[2,8,128,2,128]{4,3,2,1,0:T(2,128)(2,1)} %get-tuple-element.506, s32[1024]{0:T(1024)S(1)} %pad_clamp_fusion.3), kind=kCustom, calls=%fused_computation.clone.clone.1 | custom fusion | bytes 1048592 | tf_op jit(solution)/shard_map/while/body/eval_jaxpr/jit(_take)/gather | solution.py:96
  164.9 6.8 %fusion.138 = (f32[2,7,128]{2,1,0:T(8,128)S(1)}, f32[2,7,128,1024]{2,3,1,0:T(8,128)}) fusion(pred[128,1024]{0,1:T(8,128)(4,1)S(1)} %fusion.137, bf16[1024,2,128,1]{2,0,3,1:T(8,128)(2,1)S(1)} %bitcast.225, bf16[3,128,2,7,128]{4,1,0,3,2:T(8,128)(2,1)} %get-tuple-element.501, s32[]{:T(128)S(6)} %select_n.212), kind=kOutput, calls=%fused_computation.125.clone.1 | convolution fusion | flops 478938112 | bytes 8592388 | tf_op jit(solution)/shard_map/while/body/eval_jaxpr/sub | solution.py:29
  171.7 4.1 %fusion.139 = bf16[2,7,128,1024]{2,3,1,0:T(8,128)(2,1)S(1)} fusion(f32[2,7,128,1024]{2,3,1,0:T(8,128)} %get-tuple-element.454, f32[2,7,128]{2,1,0:T(8,128)S(1)} %get-tuple-element.455), kind=kLoop, calls=%fused_computation.16.clone.1 | loop fusion | flops 3670016 | bytes 11017216 | tf_op jit(solution)/shard_map/while/body/eval_jaxpr/convert_element_type | solution.py:32
  181.9 2.4 fusion.142
  191.8 5.1 %fusion.57 = bf16[8,2,128,2,128]{4,0,3,2,1:T(8,128)(2,1)S(1)} fusion(f32[12,2,128,2,128]{4,2,3,1,0:T(8,128)} %bitcast.231, s32[12]{0:T(128)S(1)} %copy-done.6), kind=kOutput, calls=%fused_computation.81 | convolution fusion | flops 76021856 | bytes 4194352 | tf_op jit(solution)/shard_map/ne,nxbhd->exbhd/dot_general | solution.py:128
  198.8 6.1 %all-to-all-start.1 = ((bf16[8,2,128,2,128]{4,3,2,1,0:T(2,128)(2,1)}), bf16[8,2,128,2,128]{4,3,2,1,0:T(2,128)(2,1)S(1)}, u32[]{:S(2)}, u32[]{:S(2)}) async-start(bf16[8,2,128,2,128]{4,3,2,1,0:T(2,128)(2,1)} %copy.187), calls=%async_computation.1 | async-start | bytes 2097152 | tf_op jit(solution)/shard_map/all_to_all | solution.py:129
  205.0 2.5 %collective-permute-start.1 = (bf16[2,3,128,2,128]{4,2,3,1,0:T(8,128)(2,1)S(1)}, bf16[2,3,128,2,128]{4,2,3,1,0:T(8,128)(2,1)S(1)}, u32[]{:S(2)}, u32[]{:S(2)}) collective-permute-start(bf16[2,3,128,2,128]{4,2,3,1,0:T(8,128)(2,1)S(1)} %slice.70), channel_id=1, source_target_pairs={{1,0},{2,1},{3,2},{4,3},{5,4},{6,5},{7,6},{9,8},{10,9},{11,10},{12... | collective-permute-start | bytes 1179656 | tf_op jit(solution)/shard_map/ppermute | solution.py:19
  207.4 18.7 %all-to-all-done.1 = bf16[8,2,128,2,128]{4,3,2,1,0:T(2,128)(2,1)S(1)} async-done(((bf16[8,2,128,2,128]{4,3,2,1,0:T(2,128)(2,1)}), bf16[8,2,128,2,128]{4,3,2,1,0:T(2,128)(2,1)S(1)}, u32[]{:S(2)}, u32[]{:S(2)}) %all-to-all-start.1) | async-done | bytes 1048608 | tf_op jit(solution)/shard_map/all_to_all | solution.py:129
  226.9 9.7 %collective-permute-done.1 = bf16[2,3,128,2,128]{4,2,3,1,0:T(8,128)(2,1)S(1)} collective-permute-done((bf16[2,3,128,2,128]{4,2,3,1,0:T(8,128)(2,1)S(1)}, bf16[2,3,128,2,128]{4,2,3,1,0:T(8,128)(2,1)S(1)}, u32[]{:S(2)}, u32[]{:S(2)}) %collective-permute-start.1) | collective-permute-done | bytes 393248 | tf_op jit(solution)/shard_map/ppermute | solution.py:19
  (179 shorter events, 74.1 us)
Async XLA Ops:
  26.7 0.6 copy-start.4
  29.2 11.0 %copy-start.3 = (s32[3,4]{1,0:T(4,128)S(1)}, s32[3,4]{1,0:T(4,128)}, u32[]{:S(2)}) copy-start(s32[3,4]{1,0:T(4,128)} %param.13) | copy-start | bytes 148
  31.1 33.5 %all-to-all-start = ((bf16[2,8,128,2,128]{4,2,3,0,1:T(8,128)(2,1)}), bf16[2,8,128,2,128]{4,2,3,0,1:T(8,128)(2,1)S(1)}, u32[]{:S(2)}, u32[]{:S(2)}) async-start(bf16[2,8,128,2,128]{4,2,3,0,1:T(8,128)(2,1)} %select_bitcast_fusion), calls=%async_computation | async-start | bytes 2097152 | tf_op jit(solution)/shard_map/all_to_all | solution.py:93
  36.8 26.8 %collective-permute-start = (bf16[2,3,128,2,128]{4,2,3,1,0:T(8,128)(2,1)S(1)}, bf16[2,3,128,2,128]{4,2,3,1,0:T(8,128)(2,1)S(1)}, u32[]{:S(2)}, u32[]{:S(2)}) collective-permute-start(bf16[2,3,128,2,128]{4,2,3,1,0:T(8,128)(2,1)S(1)} %copy_dynamic-update-slice_fusion), channel_id=1, source_target_pairs={{0,1},{1,2},{2,3},{3,4},{4,5},{5,6},{6,7},{8,9},{9,10},{10,11},{11... | collective-permute-start | bytes 1179656 | tf_op jit(solution)/shard_map/ppermute | solution.py:19
  41.0 27.1 %copy-start.7 = (s32[3]{0:T(128)S(1)}, s32[3]{0:T(128)}, u32[]{:S(2)}) copy-start(s32[3]{0:T(128)} %param.12) | copy-start | bytes 40
  68.1 123.7 %copy-start.6 = (s32[12]{0:T(128)S(1)}, s32[12]{0:T(128)}, u32[]{:S(2)}) copy-start(s32[12]{0:T(128)} %add_select_fusion.3) | copy-start | bytes 148
  77.8 4.1 %copy-start = (f32[2,6,128,2,128]{4,2,3,1,0:T(8,128)S(1)}, f32[2,6,128,2,128]{4,2,3,1,0:T(8,128)}, u32[]{:S(2)}) copy-start(f32[2,6,128,2,128]{4,2,3,1,0:T(8,128)} %get-tuple-element.478) | copy-start | bytes 4718596 | tf_op jit(solution)/shard_map/while
  89.2 4.1 %copy-start.2 = (bf16[3,128,2,7,128]{4,1,0,3,2:T(8,128)(2,1)S(1)}, bf16[3,128,2,7,128]{4,1,0,3,2:T(8,128)(2,1)}, u32[]{:S(2)}) copy-start(bf16[3,128,2,7,128]{4,1,0,3,2:T(8,128)(2,1)} %get-tuple-element.507) | copy-start | bytes 4128772 | tf_op jit(solution)/shard_map/while
  89.3 7.4 %slice-start = ((s8[7340032]{0:T(1024)(128)(4,1)}), s8[4194304]{0:T(1024)(128)(4,1)S(1)}, s32[]{:S(2)}) async-start(s8[7340032]{0:T(1024)(128)(4,1)} %bitcast.219), calls=%async_computation.2 | async-start | bytes 8388608 | tf_op jit(solution)/shard_map/while
  93.4 3.3 %slice-start.1 = ((s8[7340032]{0:T(1024)(128)(4,1)}), s8[3145728]{0:T(1024)(128)(4,1)S(1)}, s32[]{:S(2)}) async-start(s8[7340032]{0:T(1024)(128)(4,1)} %bitcast.219), calls=%async_computation.3 | async-start | bytes 6291456 | tf_op jit(solution)/shard_map/while
  119.1 4.1 %copy-start = (f32[2,6,128,2,128]{4,2,3,1,0:T(8,128)S(1)}, f32[2,6,128,2,128]{4,2,3,1,0:T(8,128)}, u32[]{:S(2)}) copy-start(f32[2,6,128,2,128]{4,2,3,1,0:T(8,128)} %get-tuple-element.478) | copy-start | bytes 4718596 | tf_op jit(solution)/shard_map/while
  130.5 4.1 %copy-start.2 = (bf16[3,128,2,7,128]{4,1,0,3,2:T(8,128)(2,1)S(1)}, bf16[3,128,2,7,128]{4,1,0,3,2:T(8,128)(2,1)}, u32[]{:S(2)}) copy-start(bf16[3,128,2,7,128]{4,1,0,3,2:T(8,128)(2,1)} %get-tuple-element.507) | copy-start | bytes 4128772 | tf_op jit(solution)/shard_map/while
  130.5 7.4 %slice-start = ((s8[7340032]{0:T(1024)(128)(4,1)}), s8[4194304]{0:T(1024)(128)(4,1)S(1)}, s32[]{:S(2)}) async-start(s8[7340032]{0:T(1024)(128)(4,1)} %bitcast.219), calls=%async_computation.2 | async-start | bytes 8388608 | tf_op jit(solution)/shard_map/while
  134.6 3.3 %slice-start.1 = ((s8[7340032]{0:T(1024)(128)(4,1)}), s8[3145728]{0:T(1024)(128)(4,1)S(1)}, s32[]{:S(2)}) async-start(s8[7340032]{0:T(1024)(128)(4,1)} %bitcast.219), calls=%async_computation.3 | async-start | bytes 6291456 | tf_op jit(solution)/shard_map/while
  160.3 4.1 %copy-start = (f32[2,6,128,2,128]{4,2,3,1,0:T(8,128)S(1)}, f32[2,6,128,2,128]{4,2,3,1,0:T(8,128)}, u32[]{:S(2)}) copy-start(f32[2,6,128,2,128]{4,2,3,1,0:T(8,128)} %get-tuple-element.478) | copy-start | bytes 4718596 | tf_op jit(solution)/shard_map/while
  171.7 4.1 %copy-start.2 = (bf16[3,128,2,7,128]{4,1,0,3,2:T(8,128)(2,1)S(1)}, bf16[3,128,2,7,128]{4,1,0,3,2:T(8,128)(2,1)}, u32[]{:S(2)}) copy-start(bf16[3,128,2,7,128]{4,1,0,3,2:T(8,128)(2,1)} %get-tuple-element.507) | copy-start | bytes 4128772 | tf_op jit(solution)/shard_map/while
  171.7 7.4 %slice-start = ((s8[7340032]{0:T(1024)(128)(4,1)}), s8[4194304]{0:T(1024)(128)(4,1)S(1)}, s32[]{:S(2)}) async-start(s8[7340032]{0:T(1024)(128)(4,1)} %bitcast.219), calls=%async_computation.2 | async-start | bytes 8388608 | tf_op jit(solution)/shard_map/while
  175.8 3.3 %slice-start.1 = ((s8[7340032]{0:T(1024)(128)(4,1)}), s8[3145728]{0:T(1024)(128)(4,1)S(1)}, s32[]{:S(2)}) async-start(s8[7340032]{0:T(1024)(128)(4,1)} %bitcast.219), calls=%async_computation.3 | async-start | bytes 6291456 | tf_op jit(solution)/shard_map/while
  196.9 8.0 %copy-start.1 = (f32[2,6,128,2,128]{4,2,3,1,0:T(8,128)S(1)}, f32[2,6,128,2,128]{4,2,3,1,0:T(8,128)}, u32[]{:S(2)}) copy-start(f32[2,6,128,2,128]{4,2,3,1,0:T(8,128)} %get-tuple-element.193) | copy-start | bytes 4718596
  196.9 29.3 %copy-start.5 = (s32[8]{0:T(128)S(1)}, s32[8]{0:T(128)}, u32[]{:S(2)}) copy-start(s32[8]{0:T(128)} %copy-done.4) | copy-start | bytes 100
  198.8 27.4 %all-to-all-start.1 = ((bf16[8,2,128,2,128]{4,3,2,1,0:T(2,128)(2,1)}), bf16[8,2,128,2,128]{4,3,2,1,0:T(2,128)(2,1)S(1)}, u32[]{:S(2)}, u32[]{:S(2)}) async-start(bf16[8,2,128,2,128]{4,3,2,1,0:T(2,128)(2,1)} %copy.187), calls=%async_computation.1 | async-start | bytes 2097152 | tf_op jit(solution)/shard_map/all_to_all | solution.py:129
  205.0 31.7 %collective-permute-start.1 = (bf16[2,3,128,2,128]{4,2,3,1,0:T(8,128)(2,1)S(1)}, bf16[2,3,128,2,128]{4,2,3,1,0:T(8,128)(2,1)S(1)}, u32[]{:S(2)}, u32[]{:S(2)}) collective-permute-start(bf16[2,3,128,2,128]{4,2,3,1,0:T(8,128)(2,1)S(1)} %slice.70), channel_id=1, source_target_pairs={{1,0},{2,1},{3,2},{4,3},{5,4},{6,5},{7,6},{9,8},{10,9},{11,10},{12... | collective-permute-start | bytes 1179656 | tf_op jit(solution)/shard_map/ppermute | solution.py:19
where the time goes:
time: 240 us; the launch traced here: 239 us
  local copies, waits for them, and re-layouts  55.7 us (23%)
  waiting for transfers between devices  51.1 us (21%)
  matrix products  50.7 us (21%)
  blocking collectives  25.2 us (10%)
  other arithmetic  25.1 us (10%)
  starting transfers between devices  17.6 us (7%)
  loops' own time  12.4 us (5%)
    ppermute x2, waiting for transfers between devices, shifted(): return lax.ppermute(array, axis, pairs)  32.3 us
    all_gather x1, blocking collectives, body(): all_lists = lax.all_gather(retrieved, 'seq', axis=0, tiled=True)  25.2 us
    sub x3, matrix products, attend(): weights = jnp.where(allowed[None, None], jnp.exp(scores - row_max), 0.0)  20.4 us
    all_to_all x1, waiting for transfers between devices, body(): lax.all_to_all(by_owner.astype(jnp.bfloat16), 'seq', split_axis=0, concat...  18.7 us
    dynamic_update_slice x12, local copies, waits for them, and re-layouts, body(): lax.scan(block_step, near_zero, jnp.arange(per_device, dtype=jnp.int32))  16 us
    another operation x1, loops' own time, body(): lax.scan(block_step, near_zero, jnp.arange(per_device, dtype=jnp.int32))  12.4 us
    convert_element_type x3, other arithmetic, attend(): probs_half = probs.astype(jnp.bfloat16)  12.3 us
    gather x3, local copies, waits for them, and re-layouts, fetch_memory(): return jnp.take(arrived, memory_rows // per_device, axis=1)  8.48 us
  transfers between devices with their start and end apart: 4, of which 3 were waited for; matrix products, arithmetic and copies ran while one was open for 1% of the time, Pallas kernels for 0%

commit v1 on v0

v1 whole, which is shorter than its diff:
```python
import functools
import math

import jax
import jax.numpy as jnp
from jax import lax
from jax.experimental import pallas as pl
from jax.experimental.pallas import tpu as pltpu
from jax.sharding import PartitionSpec as P

HD = 128
QH = 14
KVH = 2
GROUP = QH // KVH
BLOCK = 128
MEMORY = 4
PAD = 16
ROWS = GROUP * BLOCK
SCALE = HD ** (-0.5)
LOG2E = math.log2(math.e)

masked_score = -1e30


def shifted(array, axis, by):
    length = lax.axis_size(axis)
    pairs = [(i, i + by) for i in range(length) if 0 <= i + by < length]
    return lax.ppermute(array, axis, pairs)


def contract(a, b, dims):
    return lax.dot_general(a, b, (dims, ((), ())), preferred_element_type=jnp.float32)


def kernel(per_device, shards, own_ref, win_ref, ret_ref, q_ref, g_ref, prev_ref, kv_ref, far_ref,
           dq_ref, dprev_ref, down_ref, dfar_ref,
           wide, wide_out, qh, gh, kvs, acc, s_ref, dp_ref, dqt, slots):
    b = pl.program_id(0)
    near = 2 * per_device

    @pl.when(b == 0)
    def _():
        acc[...] = jnp.zeros_like(acc)
        kvs[0:per_device] = prev_ref[...]
        kvs[per_device:near] = kv_ref[...]
        kvs[near:near + shards] = far_ref[...]

    i = own_ref[0] * per_device + b
    earliest = i - win_ref[b]
    slots[0] = b + per_device
    count = jnp.int32(1)
    for t in range(per_device):
        j = i - per_device + t
        slots[count] = b + t
        count = count + ((j >= 0) & (j > earliest)).astype(jnp.int32)
    for r in range(MEMORY):
        e = ret_ref[b, r]
        live = e <= earliest
        for r2 in range(r):
            live = live & (e != ret_ref[b, r2])
        slots[count] = near + e // per_device
        count = count + live.astype(jnp.int32)

    flat = wide.reshape(BLOCK * PAD, HD)
    for src, dst in ((q_ref, qh), (g_ref, gh)):
        wide[:, :QH, :] = src[...].astype(jnp.float32)
        for h in range(QH):
            dst[h * BLOCK:(h + 1) * BLOCK, :] = flat[pl.ds(h, BLOCK, stride=PAD), :].astype(jnp.bfloat16)

    key_pos = lax.broadcasted_iota(jnp.int32, (BLOCK, ROWS), 0)
    query_pos = lax.broadcasted_iota(jnp.int32, (BLOCK, ROWS), 1) % BLOCK
    flat_out = wide_out.reshape(BLOCK * PAD, HD)

    def fold(x, op):
        r = x[0:8]
        for k in range(1, BLOCK // 8):
            r = op(r, x[8 * k:8 * k + 8])
        return r

    for h in range(KVH):
        head = pl.ds(h * ROWS, ROWS)

        def rows_of(n):
            return pl.ds(pl.multiple_of(n * BLOCK, BLOCK), BLOCK)

        def first(n, top):
            c = slots[n]
            s = contract(kvs[c, 0, h], qh[head, :], ((1,), (1,)))
            dp_ref[rows_of(n), :] = contract(kvs[c, 1, h], gh[head, :], ((1,), (1,)))
            return s, top

        def score(n, top):
            s, top = first(n, top)
            s_ref[rows_of(n), :] = s
            return jnp.maximum(top, fold(s, jnp.maximum))

        s, _ = first(0, None)
        s = jnp.where(key_pos <= query_pos, s, masked_score)
        s_ref[rows_of(0), :] = s
        top = lax.fori_loop(1, count, score, fold(s, jnp.maximum))
        top = jnp.max(top, axis=0, keepdims=True)

        def weigh(n, total):
            e = jnp.exp2((s_ref[rows_of(n), :] - top) * (SCALE * LOG2E))
            s_ref[rows_of(n), :] = e
            return total + fold(e, jnp.add)

        total = lax.fori_loop(0, count, weigh, jnp.zeros((8, ROWS), jnp.float32))
        inverse = 1.0 / jnp.sum(total, axis=0, keepdims=True)

        def weigh_grad(n, delta):
            p = (s_ref[rows_of(n), :] * inverse).astype(jnp.bfloat16).astype(jnp.float32)
            return delta + fold(p * dp_ref[rows_of(n), :], jnp.add)

        delta = lax.fori_loop(0, count, weigh_grad, jnp.zeros((8, ROWS), jnp.float32))
        delta = jnp.sum(delta, axis=0, keepdims=True)

        dqt[...] = jnp.zeros_like(dqt)

        def grads(n, carry):
            c = slots[n]
            p = s_ref[rows_of(n), :] * inverse
            ds = (p * (dp_ref[rows_of(n), :] - delta)).astype(jnp.bfloat16)
            acc[c, 1, h] += contract(p.astype(jnp.bfloat16), gh[head, :], ((1,), (0,)))
            acc[c, 0, h] += contract(ds, qh[head, :], ((1,), (0,)))
            dqt[...] += contract(kvs[c, 0, h], ds, ((0,), (0,)))
            return carry

        lax.fori_loop(0, count, grads, 0)
        for g in range(GROUP):
            piece = dqt[:, g * BLOCK:(g + 1) * BLOCK] * SCALE
            flat_out[pl.ds(h * GROUP + g, BLOCK, stride=PAD), :] = piece.T
    dq_ref[...] = wide_out[:, :QH, :].astype(jnp.bfloat16)

    @pl.when(b == per_device - 1)
    def _():
        for k in range(2):
            factor = SCALE if k == 0 else 1.0
            dprev_ref[:, k] = (acc[0:per_device, k] * factor).astype(jnp.bfloat16)
            down_ref[:, k] = acc[per_device:near, k] * factor
            dfar_ref[:, k] = (acc[near:near + shards, k] * factor).astype(jnp.bfloat16)


def attention_grads(own, window, retrieved, queries, output_grad, prev, kv, far):
    per_device = kv.shape[0]
    shards = far.shape[0]
    total = 2 * per_device + shards
    most = per_device + 1 + MEMORY

    def whole(shape):
        return pl.BlockSpec(shape, lambda b: (0,) * len(shape))

    smem = pl.BlockSpec(memory_space=pltpu.SMEM)
    tokens = pl.BlockSpec((BLOCK, QH, HD), lambda b: (b, 0, 0))
    half = (2, KVH, BLOCK, HD)
    return pl.pallas_call(
        functools.partial(kernel, per_device, shards),
        grid=(per_device,),
        in_specs=[smem, smem, smem, tokens, tokens, whole((per_device, *half)),
                  whole((per_device, *half)), whole((shards, *half))],
        out_specs=[tokens, whole((per_device, *half)), whole((per_device, *half)), whole((shards, *half))],
        out_shape=[
            jax.ShapeDtypeStruct(queries.shape, jnp.bfloat16),
            jax.ShapeDtypeStruct((per_device, *half), jnp.bfloat16),
            jax.ShapeDtypeStruct((per_device, *half), jnp.float32),
            jax.ShapeDtypeStruct((shards, *half), jnp.bfloat16),
        ],
        scratch_shapes=[
            pltpu.VMEM((BLOCK, PAD, HD), jnp.float32),
            pltpu.VMEM((BLOCK, PAD, HD), jnp.float32),
            pltpu.VMEM((QH * BLOCK, HD), jnp.bfloat16),
            pltpu.VMEM((QH * BLOCK, HD), jnp.bfloat16),
            pltpu.VMEM((total, *half), jnp.bfloat16),
            pltpu.VMEM((total, *half), jnp.float32),
            pltpu.VMEM((most * BLOCK, ROWS), jnp.float32),
            pltpu.VMEM((most * BLOCK, ROWS), jnp.float32),
            pltpu.VMEM((HD, ROWS), jnp.float32),
            pltpu.SMEM((most + 1,), jnp.int32),
        ],
        name="attention_grads",
    )(own, window, retrieved, queries, output_grad, prev, kv, far)


def body(queries, key_heads, value_heads, output_grad, window, retrieved):
    tokens = queries.shape[0]
    per_device = tokens // BLOCK
    shards = lax.axis_size("seq")
    own_index = lax.axis_index("seq").astype(jnp.int32)
    named = retrieved.reshape(1, per_device * MEMORY)
    owners = jnp.arange(shards, dtype=jnp.int32)[:, None]
    wants = jnp.max(jnp.where(named // per_device == owners, named % per_device, -1), axis=1)
    wanted = lax.all_to_all(wants, "seq", split_axis=0, concat_axis=0, tiled=True)

    kv = jnp.stack([key_heads, value_heads]).reshape(2, per_device, BLOCK, KVH, HD)
    kv = kv.transpose(1, 0, 3, 2, 4)
    prev = shifted(kv, "seq", 1)
    outgoing = jnp.take(kv, jnp.maximum(wanted, 0), axis=0)
    far = lax.all_to_all(outgoing, "seq", split_axis=0, concat_axis=0, tiled=True)
    query_grad, dprev, down, dfar = attention_grads(
        own_index.reshape(1), window, retrieved, queries, output_grad, prev, kv, far
    )
    replies = lax.all_to_all(dfar, "seq", split_axis=0, concat_axis=0, tiled=True)
    returned = shifted(dprev, "seq", -1).astype(jnp.float32)
    slot_hits = (wanted[:, None] == jnp.arange(per_device)[None, :]).astype(jnp.bfloat16)
    far_sum = jnp.einsum("eb,e...->b...", slot_hits, replies, preferred_element_type=jnp.float32)
    summed = (down + returned + far_sum).transpose(1, 0, 3, 2, 4).astype(jnp.bfloat16)
    summed = summed.reshape(2, tokens, KVH, HD)
    return query_grad, summed[0], summed[1]


def solution(mesh):
    rows = P(("dp", "seq"), None, None)
    return jax.shard_map(
        body,
        mesh=mesh,
        in_specs=(rows, rows, rows, rows, P(("dp", "seq")), P(("dp", "seq"), None)),
        out_specs=(rows, rows, rows),
        check_vma=False,
    )
```

time: 240 us -> 125 us (0.52)
  matrix products: 50.7 us -> 0.74 us
  local copies, waits for them, and re-layouts: 55.7 us -> 12.1 us
  Pallas kernels: 0 us -> 28.3 us
  blocking collectives: 25.2 us -> 0 us
  other arithmetic: 25.1 us -> 3.19 us
  starting transfers between devices: 17.6 us -> 30.7 us
  loops' own time: 12.4 us -> 0 us
    dot_general x17 -> x1, matrix products: 30.3 us -> 0.74 us  [body(): jnp.einsum('eb,e...->b...', slot_hits, replies, preferred_element_type=jn...]
    pallas_call x0 -> x1, Pallas kernels: none -> 28.3 us  [attention_grads(): pl.pallas_call(functools.partial(kernel, per_device, shards), grid=(per_d...]
    all_gather x1 -> x0, blocking collectives: 25.2 us -> none  [body(): all_lists = lax.all_gather(retrieved, 'seq', axis=0, tiled=True)]
    sub x3 -> x0, matrix products: 20.4 us -> none  [attend(): weights = jnp.where(allowed[None, None], jnp.exp(scores - row_max), 0.0)]
    dynamic_update_slice x18 -> x0, local copies, waits for them, and re-layouts: 20.2 us -> none  [the longest x12 16 us: body(): lax.scan(block_step, near_zero, jnp.arange(per_device, dtype=jnp.int32))]
    all_to_all x2 -> x3, starting transfers between devices: 11.8 us -> 24.8 us  [the longest x1 12.7 us: body(): lax.all_to_all(dfar, 'seq', split_axis=0, concat_axis=0, tiled=True)]
    another operation x1 -> x0, loops' own time: 12.4 us -> none  [body(): lax.scan(block_step, near_zero, jnp.arange(per_device, dtype=jnp.int32))]
    convert_element_type x3 -> x1, other arithmetic: 12.3 us -> 0.12 us  [body(): (down + returned + far_sum).transpose(1, 0, 3, 2, 4).astype(jnp.bfloat16)]
  transfers between devices with their start and end apart: 4 -> 5, of which waited for: 3 -> 4; matrix products, arithmetic and copies ran while one was open for 1% -> 7% of each run, Pallas kernels for 0% -> 0%
where the time goes in v1:
time: 125 us
  waiting for transfers between devices  49.2 us (39%)
  starting transfers between devices  30.7 us (25%)
  Pallas kernels  28.3 us (23%)
  local copies, waits for them, and re-layouts  12.1 us (10%)
  other arithmetic  3.19 us (3%)
    ppermute x2, waiting for transfers between devices, shifted(): return lax.ppermute(array, axis, pairs)  31.9 us
    pallas_call x1, Pallas kernels, attention_grads(): pl.pallas_call(functools.partial(kernel, per_device, shards), grid=(per_d...  28.3 us
    all_to_all x1, waiting for transfers between devices, body(): lax.all_to_all(dfar, 'seq', split_axis=0, concat_axis=0, tiled=True)  15.3 us
    all_to_all x1, starting transfers between devices, body(): lax.all_to_all(dfar, 'seq', split_axis=0, concat_axis=0, tiled=True)  12.7 us
    unnamed x21, local copies, waits for them, and re-layouts  8.46 us
    all_to_all x1, starting transfers between devices, body(): lax.all_to_all(wants, 'seq', split_axis=0, concat_axis=0, tiled=True)  6.22 us
    all_to_all x1, starting transfers between devices, body(): lax.all_to_all(outgoing, 'seq', split_axis=0, concat_axis=0, tiled=True)  5.96 us
    ppermute x2, starting transfers between devices, shifted(): return lax.ppermute(array, axis, pairs)  5.83 us
  transfers between devices with their start and end apart: 5, of which 4 were waited for; matrix products, arithmetic and copies ran while one was open for 7% of the time, Pallas kernels for 0%

profile of v1, /device:TPU:14, one launch (start us, length us, event | category | flops | bytes accessed | tf_op | source)
XLA Modules:
  0.0 124.9 jit_solution(16747966723896089973)
XLA Ops:
  0.6 0.7 sign_compare_fusion
  1.3 0.7 broadcast_divide_fusion
  2.4 0.7 copy.59
  3.1 6.2 %all-to-all-start = ((s32[8,1,1]{2,1,0:T(1,128)}), s32[8,1,1]{2,1,0:T(1,128)S(1)}, u32[]{:S(2)}, u32[]{:S(2)}) async-start(s32[8,1,1]{2,1,0:T(1,128)} %copy.59), calls=%async_computation | async-start | bytes 8192 | tf_op jit(solution)/shard_map/all_to_all | solution.py:192
  9.3 1.0 copy.57
  10.3 1.0 copy.58
  11.3 2.1 %all-to-all-done = s32[8,1,1]{2,1,0:T(1,128)S(1)} async-done(((s32[8,1,1]{2,1,0:T(1,128)}), s32[8,1,1]{2,1,0:T(1,128)S(1)}, u32[]{:S(2)}, u32[]{:S(2)}) %all-to-all-start) | async-done | bytes 64 | tf_op jit(solution)/shard_map/all_to_all | solution.py:192
  13.8 0.7 gather_fusion
  14.5 1.1 broadcast_select_fusion
  15.7 6.0 %all-to-all-start.1 = ((bf16[8,2,2,128,128]{4,3,2,1,0:T(8,128)(2,1)}), bf16[8,2,2,128,128]{4,3,2,1,0:T(8,128)(2,1)S(1)}, u32[]{:S(2)}, u32[]{:S(2)}) async-start(bf16[8,2,2,128,128]{4,3,2,1,0:T(8,128)(2,1)} %broadcast_select_fusion), calls=%async_computation.1 | async-start | bytes 2097152 | tf_op jit(solution)/shard_map/all_to_all | solution.py:198
  21.6 3.4 %collective-permute-start = (bf16[3,2,2,128,128]{4,3,2,1,0:T(8,128)(2,1)S(1)}, bf16[3,2,2,128,128]{4,3,2,1,0:T(8,128)(2,1)S(1)}, u32[]{:S(2)}, u32[]{:S(2)}) collective-permute-start(bf16[3,2,2,128,128]{4,3,2,1,0:T(8,128)(2,1)S(1)} %maximum_bitcast_fusion.kv_ref), channel_id=1, source_target_pairs={{0,1},{1,2},{2,3},{3,4},{4,5},{5,6},{6,7},{8,9},{9,10},{10,11},{11... | collective-permute-start | bytes 1179656 | tf_op jit(solution)/shard_map/ppermute | solution.py:28
  25.0 2.1 %copy.60.q_ref = bf16[384,14,128]{2,1,0:T(8,128)(2,1)} copy(bf16[384,14,128]{2,0,1:T(8,128)(2,1)S(1)} %copy-done.3) | data formatting | bytes 2752512 | tf_op args[0]
  27.1 2.1 %copy.61.g_ref = bf16[384,14,128]{2,1,0:T(8,128)(2,1)} copy(bf16[384,14,128]{2,0,1:T(8,128)(2,1)S(1)} %copy-done.4) | data formatting | bytes 2752512 | tf_op args[3]
  29.2 22.1 %collective-permute-done.prev_ref = bf16[3,2,2,128,128]{4,3,2,1,0:T(8,128)(2,1)S(1)} collective-permute-done((bf16[3,2,2,128,128]{4,3,2,1,0:T(8,128)(2,1)S(1)}, bf16[3,2,2,128,128]{4,3,2,1,0:T(8,128)(2,1)S(1)}, u32[]{:S(2)}, u32[]{:S(2)}) %collective-permute-start) | collective-permute-done | bytes 393248 | tf_op jit(solution)/shard_map/ppermute | solution.py:28
  51.3 0.7 copy-done.6
  52.4 28.3 %attention_grads.1 = (bf16[384,14,128]{2,1,0:T(8,128)(2,1)}, bf16[3,2,2,128,128]{4,3,2,1,0:T(8,128)(2,1)}, f32[3,2,2,128,128]{4,3,2,1,0:T(8,128)}, bf16[8,2,2,128,128]{4,3,2,1,0:T(8,128)(2,1)}) custom-call(s32[1]{0:T(128)} %bitcast.own_ref, s32[3]{0:T(128)} %win_ref.1, s32[3,4]{1,0:T(4,128)} %ret_ref.1, bf16[384,14,128]{2,1,0:T(8,128)(2,1)} %copy.60.q_ref, ...), custom_call_target="tpu_custom_call" | custom-call | tf_op jit(solution)/shard_map/attention_grads/pallas_call | solution.py:156
  80.7 12.7 %all-to-all-start.2 = ((bf16[8,2,2,128,128]{4,3,2,1,0:T(8,128)(2,1)}), bf16[8,2,2,128,128]{4,3,2,1,0:T(8,128)(2,1)S(1)}, u32[]{:S(2)}, u32[]{:S(2)}) async-start(bf16[8,2,2,128,128]{4,3,2,1,0:T(8,128)(2,1)} %get-tuple-element.10), calls=%async_computation.2 | async-start | bytes 2097152 | tf_op jit(solution)/shard_map/all_to_all | solution.py:202
  93.3 2.5 %collective-permute-start.1 = (bf16[3,2,2,128,128]{4,3,2,1,0:T(8,128)(2,1)S(1)}, bf16[3,2,2,128,128]{4,3,2,1,0:T(8,128)(2,1)S(1)}, u32[]{:S(2)}, u32[]{:S(2)}) collective-permute-start(bf16[3,2,2,128,128]{4,3,2,1,0:T(8,128)(2,1)S(1)} %copy-done.7), channel_id=1, source_target_pairs={{1,0},{2,1},{3,2},{4,3},{5,4},{6,5},{7,6},{9,8},{10,9},{11,10},{12... | collective-permute-start | bytes 1179656 | tf_op jit(solution)/shard_map/ppermute | solution.py:28
  95.8 1.4 %copy.66 = bf16[384,14,128]{2,0,1:T(8,128)(2,1)} copy(bf16[384,14,128]{2,1,0:T(8,128)(2,1)S(1)} %copy-done.2) | data formatting | bytes 2752512
  97.3 15.3 %all-to-all-done.2 = bf16[8,2,2,128,128]{4,3,2,1,0:T(8,128)(2,1)S(1)} async-done(((bf16[8,2,2,128,128]{4,3,2,1,0:T(8,128)(2,1)}), bf16[8,2,2,128,128]{4,3,2,1,0:T(8,128)(2,1)S(1)}, u32[]{:S(2)}, u32[]{:S(2)}) %all-to-all-start.2) | async-done | bytes 1048608 | tf_op jit(solution)/shard_map/all_to_all | solution.py:202
  112.5 0.7 fusion
  113.3 9.7 %collective-permute-done.1 = bf16[3,2,2,128,128]{4,3,2,1,0:T(8,128)(2,1)S(1)} collective-permute-done((bf16[3,2,2,128,128]{4,3,2,1,0:T(8,128)(2,1)S(1)}, bf16[3,2,2,128,128]{4,3,2,1,0:T(8,128)(2,1)S(1)}, u32[]{:S(2)}, u32[]{:S(2)}) %collective-permute-start.1) | collective-permute-done | bytes 393248 | tf_op jit(solution)/shard_map/ppermute | solution.py:28
  123.2 0.9 copy.68
  124.1 0.9 copy.67
  (29 shorter events, 1.4 us)
Async XLA Ops:
  3.1 10.3 %all-to-all-start = ((s32[8,1,1]{2,1,0:T(1,128)}), s32[8,1,1]{2,1,0:T(1,128)S(1)}, u32[]{:S(2)}, u32[]{:S(2)}) async-start(s32[8,1,1]{2,1,0:T(1,128)} %copy.59), calls=%async_computation | async-start | bytes 8192 | tf_op jit(solution)/shard_map/all_to_all | solution.py:192
  11.3 10.4 %copy-start = (bf16[3,2,2,128,128]{4,3,2,1,0:T(8,128)(2,1)}, bf16[3,2,2,128,128]{4,3,2,1,0:T(8,128)(2,1)S(1)}, u32[]{:S(2)}) copy-start(bf16[3,2,2,128,128]{4,3,2,1,0:T(8,128)(2,1)S(1)} %maximum_bitcast_fusion.kv_ref) | copy-start | bytes 1179652
  15.7 9.3 %copy-start.3 = (bf16[384,14,128]{2,0,1:T(8,128)(2,1)S(1)}, bf16[384,14,128]{2,0,1:T(8,128)(2,1)}, u32[]{:S(2)}) copy-start(bf16[384,14,128]{2,0,1:T(8,128)(2,1)} %param.6) | copy-start | bytes 4128772
  15.7 35.7 %all-to-all-start.1 = ((bf16[8,2,2,128,128]{4,3,2,1,0:T(8,128)(2,1)}), bf16[8,2,2,128,128]{4,3,2,1,0:T(8,128)(2,1)S(1)}, u32[]{:S(2)}, u32[]{:S(2)}) async-start(bf16[8,2,2,128,128]{4,3,2,1,0:T(8,128)(2,1)} %broadcast_select_fusion), calls=%async_computation.1 | async-start | bytes 2097152 | tf_op jit(solution)/shard_map/all_to_all | solution.py:198
  21.6 29.7 %collective-permute-start = (bf16[3,2,2,128,128]{4,3,2,1,0:T(8,128)(2,1)S(1)}, bf16[3,2,2,128,128]{4,3,2,1,0:T(8,128)(2,1)S(1)}, u32[]{:S(2)}, u32[]{:S(2)}) collective-permute-start(bf16[3,2,2,128,128]{4,3,2,1,0:T(8,128)(2,1)S(1)} %maximum_bitcast_fusion.kv_ref), channel_id=1, source_target_pairs={{0,1},{1,2},{2,3},{3,4},{4,5},{5,6},{6,7},{8,9},{9,10},{10,11},{11... | collective-permute-start | bytes 1179656 | tf_op jit(solution)/shard_map/ppermute | solution.py:28
  25.0 2.1 %copy-start.4 = (bf16[384,14,128]{2,0,1:T(8,128)(2,1)S(1)}, bf16[384,14,128]{2,0,1:T(8,128)(2,1)}, u32[]{:S(2)}) copy-start(bf16[384,14,128]{2,0,1:T(8,128)(2,1)} %param.9) | copy-start | bytes 4128772
  51.3 0.7 copy-start.6
  51.3 1.1 copy-start.1
  80.7 12.7 %copy-start.7 = (bf16[3,2,2,128,128]{4,3,2,1,0:T(8,128)(2,1)S(1)}, bf16[3,2,2,128,128]{4,3,2,1,0:T(8,128)(2,1)}, u32[]{:S(2)}) copy-start(bf16[3,2,2,128,128]{4,3,2,1,0:T(8,128)(2,1)} %get-tuple-element.9) | copy-start | bytes 1179652
  80.7 15.1 %copy-start.2 = (bf16[384,14,128]{2,1,0:T(8,128)(2,1)S(1)}, bf16[384,14,128]{2,1,0:T(8,128)(2,1)}, u32[]{:S(2)}) copy-start(bf16[384,14,128]{2,1,0:T(8,128)(2,1)} %get-tuple-element.23) | copy-start | bytes 4128772
  80.7 31.8 %all-to-all-start.2 = ((bf16[8,2,2,128,128]{4,3,2,1,0:T(8,128)(2,1)}), bf16[8,2,2,128,128]{4,3,2,1,0:T(8,128)(2,1)S(1)}, u32[]{:S(2)}, u32[]{:S(2)}) async-start(bf16[8,2,2,128,128]{4,3,2,1,0:T(8,128)(2,1)} %get-tuple-element.10), calls=%async_computation.2 | async-start | bytes 2097152 | tf_op jit(solution)/shard_map/all_to_all | solution.py:202
  93.3 29.6 %collective-permute-start.1 = (bf16[3,2,2,128,128]{4,3,2,1,0:T(8,128)(2,1)S(1)}, bf16[3,2,2,128,128]{4,3,2,1,0:T(8,128)(2,1)S(1)}, u32[]{:S(2)}, u32[]{:S(2)}) collective-permute-start(bf16[3,2,2,128,128]{4,3,2,1,0:T(8,128)(2,1)S(1)} %copy-done.7), channel_id=1, source_target_pairs={{1,0},{2,1},{3,2},{4,3},{5,4},{6,5},{7,6},{9,8},{10,9},{11,10},{12... | collective-permute-start | bytes 1179656 | tf_op jit(solution)/shard_map/ppermute | solution.py:28
  97.3 25.7 %copy-start.5 = (f32[3,2,2,128,128]{4,3,2,1,0:T(8,128)S(1)}, f32[3,2,2,128,128]{4,3,2,1,0:T(8,128)}, u32[]{:S(2)}) copy-start(f32[3,2,2,128,128]{4,3,2,1,0:T(8,128)} %get-tuple-element.8) | copy-start | bytes 2359300

commit v2 on v1

v2 whole, which is shorter than its diff:
```python
import functools
import math

import jax
import jax.numpy as jnp
from jax import lax
from jax.experimental import pallas as pl
from jax.experimental.pallas import tpu as pltpu
from jax.sharding import PartitionSpec as P


HD = 128
QH = 14
KVH = 2
GROUP = QH // KVH
BLOCK = 128
SLAB = 16
MEMORY = 4
ROWS = GROUP * BLOCK
SCALE = HD ** (-0.5)
LOG2E = math.log2(math.e)

masked_score = -1e30


def contract(a, b, dims):
    return lax.dot_general(a, b, (dims, ((), ())), preferred_element_type=jnp.float32)


def fold(x, op):
    r = x[0:8]
    for k in range(1, x.shape[0] // 8):
        r = op(r, x[8 * k:8 * k + 8])
    return r


def list_near(per_device, b, own_ref, win_ref, slots):
    i = own_ref[0] * per_device + b
    earliest = i - win_ref[b]
    slots[0] = b + per_device
    count = jnp.int32(1)
    for back in range(1, per_device + 1):
        j = i - back
        slots[count] = b + per_device - back
        count = count + ((j >= 0) & (j > earliest)).astype(jnp.int32)
    return earliest, count


def list_far(per_device, b, ret_ref, earliest, count, slots):
    for r in range(MEMORY):
        e = ret_ref[b, r]
        live = e <= earliest
        for r2 in range(r):
            live = live & (e != ret_ref[b, r2])
        slots[count] = 2 * per_device + e // per_device
        count = count + live.astype(jnp.int32)
    return count


def weigh(s, top):
    return jnp.exp2((s - top) * (SCALE * LOG2E))


def kernel(per_device, shards, h, own_ref, win_ref, ret_ref, q_ref, g_ref, prev_ref, kv_ref, far_ref, *refs):
    if h > 0:
        refs = refs[2:]
    dq_ref, down_ref, dprev_ref, dfar_ref, kvs, acc, s_ref, dp_ref, dqt, slots = refs
    b = pl.program_id(0)
    near = 2 * per_device

    @pl.when(b == 0)
    def _():
        acc[...] = jnp.zeros_like(acc)
        kvs[0:per_device] = prev_ref[0]
        kvs[per_device:near] = kv_ref[0]
        kvs[near:near + shards] = far_ref[...]

    earliest, count = list_near(per_device, b, own_ref, win_ref, slots)
    count = list_far(per_device, b, ret_ref, earliest, count, slots)
    qh = q_ref.reshape(ROWS, HD)
    gh = g_ref.reshape(ROWS, HD)

    def each(body, first, stop, carry, width=2):
        whole = (stop - first) // width

        def wide(m, c):
            return body(first + m * width, width, c)

        carry = lax.fori_loop(0, whole, wide, carry)
        return lax.fori_loop(first + whole * width, stop, lambda n, c: body(n, 1, c), carry)

    def rows_at(n, width):
        return pl.ds(pl.multiple_of(n * BLOCK, BLOCK), width * BLOCK)

    def blocks(n, width, which):
        return jnp.concatenate([kvs[slots[n + k], which] for k in range(width)], axis=0)

    def products(n, width):
        dp_ref[rows_at(n, width), :] = contract(blocks(n, width, 1), gh[...], ((1,), (1,)))
        return contract(blocks(n, width, 0), qh[...], ((1,), (1,)))

    def score(n, width, top):
        s = products(n, width)
        s_ref[rows_at(n, width), :] = s
        return jnp.maximum(top, fold(s, jnp.maximum))

    key_pos = lax.broadcasted_iota(jnp.int32, (BLOCK, ROWS), 0)
    query_pos = lax.broadcasted_iota(jnp.int32, (BLOCK, ROWS), 1) % BLOCK
    s = jnp.where(key_pos <= query_pos, products(0, 1), masked_score)
    s_ref[rows_at(0, 1), :] = s
    top = each(score, 1, count, fold(s, jnp.maximum))
    top = jnp.max(top, axis=0, keepdims=True)

    def slab(n, k):
        return pl.ds(pl.multiple_of(n * BLOCK, BLOCK) + k * SLAB, SLAB)

    def weigh_one(n, total):
        e = weigh(s_ref[rows_at(n, 1), :], top)
        s_ref[rows_at(n, 1), :] = e
        return total + fold(e, jnp.add)

    total = lax.fori_loop(0, count, weigh_one, jnp.zeros((8, ROWS), jnp.float32))
    inverse = 1.0 / jnp.sum(total, axis=0, keepdims=True)

    def weigh_grad(n, delta):
        for k in range(BLOCK // SLAB):
            p = (s_ref[slab(n, k), :] * inverse).astype(jnp.bfloat16).astype(jnp.float32)
            delta = delta + fold(p * dp_ref[slab(n, k), :], jnp.add)
        return delta

    delta = lax.fori_loop(0, count, weigh_grad, jnp.zeros((8, ROWS), jnp.float32))
    delta = jnp.sum(delta, axis=0, keepdims=True)
    dqt[...] = jnp.zeros_like(dqt)

    def grads(n, width, carry):
        p = s_ref[rows_at(n, width), :] * inverse
        ds = (p * (dp_ref[rows_at(n, width), :] - delta)).astype(jnp.bfloat16)
        value_terms = contract(p.astype(jnp.bfloat16), gh[...], ((1,), (0,)))
        key_terms = contract(ds, qh[...], ((1,), (0,)))
        for k in range(width):
            c = slots[n + k]
            acc[c, 1] += value_terms[k * BLOCK:(k + 1) * BLOCK]
            acc[c, 0] += key_terms[k * BLOCK:(k + 1) * BLOCK]
        dqt[...] += contract(blocks(n, width, 0), ds, ((0,), (0,)))
        return carry

    each(grads, 0, count, 0)
    for g in range(GROUP):
        piece = dqt[:, g * BLOCK:(g + 1) * BLOCK] * SCALE
        dq_ref[g] = piece.T.astype(jnp.bfloat16)

    @pl.when(b == per_device - 1)
    def _():
        for k in range(2):
            factor = SCALE if k == 0 else 1.0
            dprev_ref[:, k] = (acc[0:per_device, k] * factor).astype(jnp.bfloat16)
            down_ref[0, :, k] = acc[per_device:near, k] * factor
            dfar_ref[:, k] = (acc[near:near + shards, k] * factor).astype(jnp.bfloat16)


def attention_grads(h, own, window, retrieved, queries, output_grad, prev, kv, far, *carried):
    per_device = kv.shape[1]
    shards = far.shape[0]
    total = 2 * per_device + shards
    most = per_device + 1 + MEMORY
    pair = (2, BLOCK, HD)
    smem = pl.BlockSpec(memory_space=pltpu.SMEM)
    tokens = pl.BlockSpec((GROUP, BLOCK, HD), lambda b: (h, b, 0))
    of_head = pl.BlockSpec((1, per_device, *pair), lambda b: (h, 0, 0, 0, 0))
    of_owner = pl.BlockSpec((shards, *pair), lambda b: (0, 0, 0, 0))
    return pl.pallas_call(
        functools.partial(kernel, per_device, shards, h),
        grid=(per_device,),
        in_specs=[smem, smem, smem, tokens, tokens, of_head, of_head, of_owner]
        + [pl.BlockSpec(memory_space=pl.ANY)] * len(carried),
        out_specs=[tokens, of_head, pl.BlockSpec((per_device, *pair), lambda b: (0, 0, 0, 0)), of_owner],
        out_shape=[
            jax.ShapeDtypeStruct(queries.shape, jnp.bfloat16),
            jax.ShapeDtypeStruct((KVH, per_device, *pair), jnp.float32),
            jax.ShapeDtypeStruct((per_device, *pair), jnp.bfloat16),
            jax.ShapeDtypeStruct((shards, *pair), jnp.bfloat16),
        ],
        scratch_shapes=[
            pltpu.VMEM((total, *pair), jnp.bfloat16),
            pltpu.VMEM((total, *pair), jnp.float32),
            pltpu.VMEM((most * BLOCK, ROWS), jnp.float32),
            pltpu.VMEM((most * BLOCK, ROWS), jnp.float32),
            pltpu.VMEM((HD, ROWS), jnp.float32),
            pltpu.SMEM((most + 1,), jnp.int32),
        ],
        input_output_aliases={8: 0, 9: 1} if carried else {},
        cost_estimate=pl.CostEstimate(
            flops=10 * per_device * most * BLOCK * ROWS * HD,
            transcendentals=per_device * most * BLOCK * ROWS,
            bytes_accessed=8 * queries.size,
        ),
    )(own, window, retrieved, queries, output_grad, prev, kv, far, *carried)


def exchange(array):
    return lax.all_to_all(array, "seq", split_axis=0, concat_axis=0, tiled=True)


def shifted(array, by):
    length = lax.axis_size("seq")
    pairs = [(i, i + by) for i in range(length) if 0 <= i + by < length]
    return lax.ppermute(array, "seq", pairs)


def body(queries, key_heads, value_heads, output_grad, window, retrieved):
    tokens = queries.shape[0]
    per_device = tokens // BLOCK
    shards = lax.axis_size("seq")
    own_index = lax.axis_index("seq").astype(jnp.int32).reshape(1)
    named = retrieved.reshape(1, per_device * MEMORY)
    owners = jnp.arange(shards, dtype=jnp.int32)[:, None]
    wants = jnp.max(jnp.where(named // per_device == owners, named % per_device, -1), axis=1)
    wanted = exchange(wants)

    kv = jnp.stack([key_heads, value_heads]).reshape(2, per_device, BLOCK, KVH, HD)
    kv = kv.transpose(3, 1, 0, 2, 4)
    prev = shifted(kv, 1)
    slot_hits = (wanted[:, None] == jnp.arange(per_device)[None, :]).astype(jnp.bfloat16)
    queries = queries.transpose(1, 0, 2)
    output_grad = output_grad.transpose(1, 0, 2)
    carried = ()
    fars = []
    replies = []
    returned = []
    for h in range(KVH):
        outgoing = jnp.take(kv[h], jnp.maximum(wanted, 0), axis=0, mode="clip")
        fars.append(exchange(outgoing))
    for h in range(KVH):
        *carried, dprev, dfar = attention_grads(
            h, own_index, window, retrieved, queries, output_grad, prev, kv, fars[h], *carried
        )
        replies.append(exchange(dfar))
        returned.append(shifted(dprev, -1).astype(jnp.float32))
    query_grad, down = carried
    sums = []
    for h in range(KVH):
        far_sum = jnp.einsum(
            "eb,e...->b...", slot_hits, replies[h], preferred_element_type=jnp.float32
        )
        sums.append(down[h] + returned[h] + far_sum)
    summed = jnp.stack(sums).transpose(2, 1, 3, 0, 4).astype(jnp.bfloat16)
    summed = summed.reshape(2, tokens, KVH, HD)
    return query_grad.transpose(1, 0, 2), summed[0], summed[1]


def solution(mesh):
    rows = P(("dp", "seq"), None, None)
    return jax.shard_map(
        body,
        mesh=mesh,
        in_specs=(rows, rows, rows, rows, P(("dp", "seq")), P(("dp", "seq"), None)),
        out_specs=(rows, rows, rows),
        check_vma=False,
    )
```

time: 125 us -> 134 us (1.072); the launches traced: 125 us -> 131 us
  blocking collectives: 0 us -> 23 us
  waiting for transfers between devices: 49.2 us -> 41.1 us
  Pallas kernels: 28.3 us -> 21 us
  local copies, waits for them, and re-layouts: 12.1 us -> 9.05 us
  starting transfers between devices: 30.7 us -> 33.6 us
    all_to_all x0 -> x1, blocking collectives: none -> 23 us  [exchange(): return lax.all_to_all(array, 'seq', split_axis=0, concat_axis=0, tiled=True)]
    pallas_call x1 -> x2, Pallas kernels: 28.3 us -> 21 us  [attention_grads(): pl.pallas_call(functools.partial(kernel, per_device, shards, h), grid=(pe...]
    ppermute x2 -> x3, waiting for transfers between devices: 31.9 us -> 25 us  [shifted(): return lax.ppermute(array, 'seq', pairs)]
    ppermute x2 -> x3, starting transfers between devices: 5.83 us -> 9.19 us  [shifted(): return lax.ppermute(array, 'seq', pairs)]
    unnamed x21 -> x18, local copies, waits for them, and re-layouts: 8.46 us -> 5.25 us
    gather x1 -> x2, local copies, waits for them, and re-layouts: 0.75 us -> 2.82 us  [body(): outgoing = jnp.take(kv[h], jnp.maximum(wanted, 0), axis=0, mode='clip')]
    another operation x2 -> x0, local copies, waits for them, and re-layouts: 1.91 us -> none  [body(): jnp.stack([key_heads, value_heads]).reshape(2, per_device, BLOCK, KVH, HD)]
    all_to_all x3 -> x4, waiting for transfers between devices: 17.4 us -> 16 us  [exchange(): return lax.all_to_all(array, 'seq', split_axis=0, concat_axis=0, tiled=True)]
  transfers between devices with their start and end apart: 5 -> 7, of which waited for: 4 -> 6; matrix products, arithmetic and copies ran while one was open for 7% -> 3% of each run, Pallas kernels for 0% -> 8%
where the time goes in v2:
time: 134 us; the launch traced here: 131 us
  waiting for transfers between devices  41.1 us (31%)
  starting transfers between devices  33.6 us (25%)
  blocking collectives  23 us (17%)
  Pallas kernels  21 us (16%)
  local copies, waits for them, and re-layouts  9.05 us (7%)
  other arithmetic  2.09 us (2%)
    ppermute x3, waiting for transfers between devices, shifted(): return lax.ppermute(array, 'seq', pairs)  25 us
    all_to_all x4, starting transfers between devices, exchange(): return lax.all_to_all(array, 'seq', split_axis=0, concat_axis=0, tiled=True)  24.4 us
    all_to_all x1, blocking collectives, exchange(): return lax.all_to_all(array, 'seq', split_axis=0, concat_axis=0, tiled=True)  23 us
    pallas_call x2, Pallas kernels, attention_grads(): pl.pallas_call(functools.partial(kernel, per_device, shards, h), grid=(pe...  21 us
    all_to_all x4, waiting for transfers between devices, exchange(): return lax.all_to_all(array, 'seq', split_axis=0, concat_axis=0, tiled=True)  16 us
    ppermute x3, starting transfers between devices, shifted(): return lax.ppermute(array, 'seq', pairs)  9.19 us
    unnamed x18, local copies, waits for them, and re-layouts  5.25 us
    gather x2, local copies, waits for them, and re-layouts, body(): outgoing = jnp.take(kv[h], jnp.maximum(wanted, 0), axis=0, mode='clip')  2.82 us
  transfers between devices with their start and end apart: 7, of which 6 were waited for; matrix products, arithmetic and copies ran while one was open for 3% of the time, Pallas kernels for 8%

profile of v2, /device:TPU:14, one launch (start us, length us, event | category | flops | bytes accessed | tf_op | source)
XLA Modules:
  0.0 131.5 jit_solution(4153347661124849497)
XLA Ops:
  3.1 6.2 %all-to-all-start = ((s32[8,1,1]{2,1,0:T(1,128)}), s32[8,1,1]{2,1,0:T(1,128)S(1)}, u32[]{:S(2)}, u32[]{:S(2)}) async-start(s32[8,1,1]{2,1,0:T(1,128)} %copy.39), calls=%async_computation | async-start | bytes 8192 | tf_op jit(solution)/shard_map/all_to_all | solution.py:201
  9.3 1.0 copy.37
  10.3 1.0 copy.38
  11.3 2.1 %all-to-all-done = s32[8,1,1]{2,1,0:T(1,128)S(1)} async-done(((s32[8,1,1]{2,1,0:T(1,128)}), s32[8,1,1]{2,1,0:T(1,128)S(1)}, u32[]{:S(2)}, u32[]{:S(2)}) %all-to-all-start) | async-done | bytes 64 | tf_op jit(solution)/shard_map/all_to_all | solution.py:201
  13.7 1.4 %gather_fusion.1 = bf16[8,2,128,128]{3,2,1,0:T(8,128)(2,1)} fusion(bf16[3,2,128,128]{3,2,1,0:T(8,128)(2,1)S(1)} %get-tuple-element.37, s32[1024]{0:T(1024)S(1)} %pad_clamp_fusion), kind=kCustom, calls=%fused_computation.1 | custom fusion | bytes 1048608 | tf_op jit(solution)/shard_map/jit(_take)/gather | solution.py:231
  15.2 5.8 %all-to-all-start.2 = ((bf16[8,2,128,128]{3,2,1,0:T(8,128)(2,1)}), bf16[8,2,128,128]{3,2,1,0:T(8,128)(2,1)S(1)}, u32[]{:S(2)}, u32[]{:S(2)}) async-start(bf16[8,2,128,128]{3,2,1,0:T(8,128)(2,1)} %gather_fusion.1), calls=%async_computation.2 | async-start | bytes 1048576 | tf_op jit(solution)/shard_map/all_to_all | solution.py:201
  20.9 1.4 %gather_fusion = bf16[8,2,128,128]{3,2,1,0:T(8,128)(2,1)} fusion(bf16[3,2,128,128]{3,2,1,0:T(8,128)(2,1)S(1)} %get-tuple-element.38, s32[1024]{0:T(1024)S(1)} %pad_clamp_fusion), kind=kCustom, calls=%fused_computation | custom fusion | bytes 1048608 | tf_op jit(solution)/shard_map/jit(_take)/gather | solution.py:231
  22.3 9.1 %all-to-all-done.2.far_ref = bf16[8,2,128,128]{3,2,1,0:T(8,128)(2,1)S(1)} async-done(((bf16[8,2,128,128]{3,2,1,0:T(8,128)(2,1)}), bf16[8,2,128,128]{3,2,1,0:T(8,128)(2,1)S(1)}, u32[]{:S(2)}, u32[]{:S(2)}) %all-to-all-start.2) | async-done | bytes 524320 | tf_op jit(solution)/shard_map/all_to_all | solution.py:201
  31.4 6.5 %all-to-all-start.1 = ((bf16[8,2,128,128]{3,2,1,0:T(8,128)(2,1)}), bf16[8,2,128,128]{3,2,1,0:T(8,128)(2,1)S(1)}, u32[]{:S(2)}, u32[]{:S(2)}) async-start(bf16[8,2,128,128]{3,2,1,0:T(8,128)(2,1)} %gather_fusion), calls=%async_computation.1 | async-start | bytes 1048576 | tf_op jit(solution)/shard_map/all_to_all | solution.py:201
  37.9 3.4 %collective-permute-start = (bf16[2,3,2,128,128]{4,3,2,1,0:T(8,128)(2,1)S(1)}, bf16[2,3,2,128,128]{4,3,2,1,0:T(8,128)(2,1)S(1)}, u32[]{:S(2)}, u32[]{:S(2)}) collective-permute-start(bf16[2,3,2,128,128]{4,3,2,1,0:T(8,128)(2,1)S(1)} %maximum_bitcast_fusion.kv_ref), channel_id=1, source_target_pairs={{0,1},{1,2},{2,3},{3,4},{4,5},{5,6},{6,7},{8,9},{9,10},{10,11},{11... | collective-permute-start | bytes 1179656 | tf_op jit(solution)/shard_map/ppermute | solution.py:207
  41.3 15.5 %collective-permute-done.prev_ref = bf16[2,3,2,128,128]{4,3,2,1,0:T(8,128)(2,1)S(1)} collective-permute-done((bf16[2,3,2,128,128]{4,3,2,1,0:T(8,128)(2,1)S(1)}, bf16[2,3,2,128,128]{4,3,2,1,0:T(8,128)(2,1)S(1)}, u32[]{:S(2)}, u32[]{:S(2)}) %collective-permute-start) | collective-permute-done | bytes 393248 | tf_op jit(solution)/shard_map/ppermute | solution.py:207
  56.8 0.8 copy-done.4
  57.6 10.5 %shard_map.85 = (bf16[14,384,128]{2,1,0:T(8,128)(2,1)}, f32[2,3,2,128,128]{4,3,2,1,0:T(8,128)}, bf16[3,2,128,128]{3,2,1,0:T(8,128)(2,1)}, bf16[8,2,128,128]{3,2,1,0:T(8,128)(2,1)}) custom-call(s32[1]{0:T(128)} %bitcast.own_ref, s32[3]{0:T(128)} %win_ref.3, s32[3,4]{1,0:T(4,128)} %ret_ref.3, bf16[14,384,128]{2,1,0:T(8,128)(2,1)} %bitcast.48, ...), custom_call_target="tpu_custom_call" | custom-call | flops 3523215360 | bytes 5505024 | tf_op jit(solution)/shard_map/pallas_call | solution.py:171
  68.1 0.8 copy-done.3
  68.9 10.5 %shard_map.86 = (bf16[14,384,128]{2,1,0:T(8,128)(2,1)}, f32[2,3,2,128,128]{4,3,2,1,0:T(8,128)}, bf16[3,2,128,128]{3,2,1,0:T(8,128)(2,1)}, bf16[8,2,128,128]{3,2,1,0:T(8,128)(2,1)}) custom-call(s32[1]{0:T(128)} %bitcast.own_ref, s32[3]{0:T(128)} %win_ref.3, s32[3,4]{1,0:T(4,128)} %ret_ref.3, ...), custom_call_target="tpu_custom_call", output_to_operand_aliasing={{0}: (8, {}), {1}: (9, {})} | custom-call | flops 3523215360 | bytes 5505024 | tf_op jit(solution)/shard_map/pallas_call | solution.py:171
  79.5 23.0 %all_to_all.29 = bf16[8,2,128,128]{3,2,1,0:T(8,128)(2,1)S(1)} all-to-all(bf16[8,2,128,128]{3,2,1,0:T(8,128)(2,1)} %get-tuple-element.18), channel_id=1, replica_groups=mesh['dp'=4,'seq'=8] {'seq'}, dimensions={0} | all-to-all | bytes 1048576 | tf_op jit(solution)/shard_map/all_to_all | solution.py:201
  102.5 5.9 %all-to-all-start.3 = ((bf16[8,2,128,128]{3,2,1,0:T(8,128)(2,1)}), bf16[8,2,128,128]{3,2,1,0:T(8,128)(2,1)S(1)}, u32[]{:S(2)}, u32[]{:S(2)}) async-start(bf16[8,2,128,128]{3,2,1,0:T(8,128)(2,1)} %get-tuple-element.16), calls=%async_computation.3 | async-start | bytes 1048576 | tf_op jit(solution)/shard_map/all_to_all | solution.py:201
  108.4 2.5 %collective-permute-start.2 = (bf16[3,2,128,128]{3,2,1,0:T(8,128)(2,1)S(1)}, bf16[3,2,128,128]{3,2,1,0:T(8,128)(2,1)S(1)}, u32[]{:S(2)}, u32[]{:S(2)}) collective-permute-start(bf16[3,2,128,128]{3,2,1,0:T(8,128)(2,1)S(1)} %copy-done.6), channel_id=1, source_target_pairs={{1,0},{2,1},{3,2},{4,3},{5,4},{6,5},{7,6},{9,8},{10,9},{11,10},{12... | collective-permute-start | bytes 589832 | tf_op jit(solution)/shard_map/ppermute | solution.py:207
  110.9 3.4 %collective-permute-start.1 = (bf16[3,2,128,128]{3,2,1,0:T(8,128)(2,1)S(1)}, bf16[3,2,128,128]{3,2,1,0:T(8,128)(2,1)S(1)}, u32[]{:S(2)}, u32[]{:S(2)}) collective-permute-start(bf16[3,2,128,128]{3,2,1,0:T(8,128)(2,1)S(1)} %copy-done.5), channel_id=1, source_target_pairs={{1,0},{2,1},{3,2},{4,3},{5,4},{6,5},{7,6},{9,8},{10,9},{11,10},{12... | collective-permute-start | bytes 589832 | tf_op jit(solution)/shard_map/ppermute | solution.py:207
  114.7 4.9 %all-to-all-done.3 = bf16[8,2,128,128]{3,2,1,0:T(8,128)(2,1)S(1)} async-done(((bf16[8,2,128,128]{3,2,1,0:T(8,128)(2,1)}), bf16[8,2,128,128]{3,2,1,0:T(8,128)(2,1)S(1)}, u32[]{:S(2)}, u32[]{:S(2)}) %all-to-all-start.3) | async-done | bytes 524320 | tf_op jit(solution)/shard_map/all_to_all | solution.py:201
  120.0 7.0 %collective-permute-done.2 = bf16[3,2,128,128]{3,2,1,0:T(8,128)(2,1)S(1)} collective-permute-done((bf16[3,2,128,128]{3,2,1,0:T(8,128)(2,1)S(1)}, bf16[3,2,128,128]{3,2,1,0:T(8,128)(2,1)S(1)}, u32[]{:S(2)}, u32[]{:S(2)}) %collective-permute-start.2) | collective-permute-done | bytes 196640 | tf_op jit(solution)/shard_map/ppermute | solution.py:207
  127.0 2.5 %collective-permute-done.1 = bf16[3,2,128,128]{3,2,1,0:T(8,128)(2,1)S(1)} collective-permute-done((bf16[3,2,128,128]{3,2,1,0:T(8,128)(2,1)S(1)}, bf16[3,2,128,128]{3,2,1,0:T(8,128)(2,1)S(1)}, u32[]{:S(2)}, u32[]{:S(2)}) %collective-permute-start.1) | collective-permute-done | bytes 196640 | tf_op jit(solution)/shard_map/ppermute | solution.py:207
  129.7 0.9 copy.45
  130.6 0.9 copy.44
  (30 shorter events, 3.9 us)
Async XLA Ops:
  3.1 10.3 %all-to-all-start = ((s32[8,1,1]{2,1,0:T(1,128)}), s32[8,1,1]{2,1,0:T(1,128)S(1)}, u32[]{:S(2)}, u32[]{:S(2)}) async-start(s32[8,1,1]{2,1,0:T(1,128)} %copy.39), calls=%async_computation | async-start | bytes 8192 | tf_op jit(solution)/shard_map/all_to_all | solution.py:201
  11.3 26.7 %copy-start = (bf16[2,3,2,128,128]{4,3,2,1,0:T(8,128)(2,1)}, bf16[2,3,2,128,128]{4,3,2,1,0:T(8,128)(2,1)S(1)}, u32[]{:S(2)}) copy-start(bf16[2,3,2,128,128]{4,3,2,1,0:T(8,128)(2,1)S(1)} %maximum_bitcast_fusion.kv_ref) | copy-start | bytes 1179652
  15.2 16.3 %all-to-all-start.2 = ((bf16[8,2,128,128]{3,2,1,0:T(8,128)(2,1)}), bf16[8,2,128,128]{3,2,1,0:T(8,128)(2,1)S(1)}, u32[]{:S(2)}, u32[]{:S(2)}) async-start(bf16[8,2,128,128]{3,2,1,0:T(8,128)(2,1)} %gather_fusion.1), calls=%async_computation.2 | async-start | bytes 1048576 | tf_op jit(solution)/shard_map/all_to_all | solution.py:201
  31.4 25.4 %copy-start.2 = (bf16[8,2,128,128]{3,2,1,0:T(8,128)(2,1)}, bf16[8,2,128,128]{3,2,1,0:T(8,128)(2,1)S(1)}, u32[]{:S(2)}) copy-start(bf16[8,2,128,128]{3,2,1,0:T(8,128)(2,1)S(1)} %all-to-all-done.2.far_ref) | copy-start | bytes 1572868
  31.4 36.7 %all-to-all-start.1 = ((bf16[8,2,128,128]{3,2,1,0:T(8,128)(2,1)}), bf16[8,2,128,128]{3,2,1,0:T(8,128)(2,1)S(1)}, u32[]{:S(2)}, u32[]{:S(2)}) async-start(bf16[8,2,128,128]{3,2,1,0:T(8,128)(2,1)} %gather_fusion), calls=%async_computation.1 | async-start | bytes 1048576 | tf_op jit(solution)/shard_map/all_to_all | solution.py:201
  37.9 18.9 %collective-permute-start = (bf16[2,3,2,128,128]{4,3,2,1,0:T(8,128)(2,1)S(1)}, bf16[2,3,2,128,128]{4,3,2,1,0:T(8,128)(2,1)S(1)}, u32[]{:S(2)}, u32[]{:S(2)}) collective-permute-start(bf16[2,3,2,128,128]{4,3,2,1,0:T(8,128)(2,1)S(1)} %maximum_bitcast_fusion.kv_ref), channel_id=1, source_target_pairs={{0,1},{1,2},{2,3},{3,4},{4,5},{5,6},{6,7},{8,9},{9,10},{10,11},{11... | collective-permute-start | bytes 1179656 | tf_op jit(solution)/shard_map/ppermute | solution.py:207
  56.8 0.8 copy-start.4
  68.1 0.8 copy-start.3
  79.4 29.0 %copy-start.6 = (bf16[3,2,128,128]{3,2,1,0:T(8,128)(2,1)S(1)}, bf16[3,2,128,128]{3,2,1,0:T(8,128)(2,1)}, u32[]{:S(2)}) copy-start(bf16[3,2,128,128]{3,2,1,0:T(8,128)(2,1)} %get-tuple-element.17) | copy-start | bytes 589828
  79.4 31.5 %copy-start.5 = (bf16[3,2,128,128]{3,2,1,0:T(8,128)(2,1)S(1)}, bf16[3,2,128,128]{3,2,1,0:T(8,128)(2,1)}, u32[]{:S(2)}) copy-start(bf16[3,2,128,128]{3,2,1,0:T(8,128)(2,1)} %get-tuple-element.15) | copy-start | bytes 589828
  102.5 27.0 %copy-start.1 = (f32[2,3,2,128,128]{4,3,2,1,0:T(8,128)S(1)}, f32[2,3,2,128,128]{4,3,2,1,0:T(8,128)}, u32[]{:S(2)}) copy-start(f32[2,3,2,128,128]{4,3,2,1,0:T(8,128)} %get-tuple-element.14) | copy-start | bytes 2359300
  102.5 17.1 %all-to-all-start.3 = ((bf16[8,2,128,128]{3,2,1,0:T(8,128)(2,1)}), bf16[8,2,128,128]{3,2,1,0:T(8,128)(2,1)S(1)}, u32[]{:S(2)}, u32[]{:S(2)}) async-start(bf16[8,2,128,128]{3,2,1,0:T(8,128)(2,1)} %get-tuple-element.16), calls=%async_computation.3 | async-start | bytes 1048576 | tf_op jit(solution)/shard_map/all_to_all | solution.py:201
  108.4 18.6 %collective-permute-start.2 = (bf16[3,2,128,128]{3,2,1,0:T(8,128)(2,1)S(1)}, bf16[3,2,128,128]{3,2,1,0:T(8,128)(2,1)S(1)}, u32[]{:S(2)}, u32[]{:S(2)}) collective-permute-start(bf16[3,2,128,128]{3,2,1,0:T(8,128)(2,1)S(1)} %copy-done.6), channel_id=1, source_target_pairs={{1,0},{2,1},{3,2},{4,3},{5,4},{6,5},{7,6},{9,8},{10,9},{11,10},{12... | collective-permute-start | bytes 589832 | tf_op jit(solution)/shard_map/ppermute | solution.py:207
  110.9 18.6 %collective-permute-start.1 = (bf16[3,2,128,128]{3,2,1,0:T(8,128)(2,1)S(1)}, bf16[3,2,128,128]{3,2,1,0:T(8,128)(2,1)S(1)}, u32[]{:S(2)}, u32[]{:S(2)}) collective-permute-start(bf16[3,2,128,128]{3,2,1,0:T(8,128)(2,1)S(1)} %copy-done.5), channel_id=1, source_target_pairs={{1,0},{2,1},{3,2},{4,3},{5,4},{6,5},{7,6},{9,8},{10,9},{11,10},{12... | collective-permute-start | bytes 589832 | tf_op jit(solution)/shard_map/ppermute | solution.py:207

commit v3 on v2

--- a/solution.py
+++ b/solution.py
@@ -57,10 +57,6 @@
     return count
 
 
-def weigh(s, top):
-    return jnp.exp2((s - top) * (SCALE * LOG2E))
-
-
 def kernel(per_device, shards, h, own_ref, win_ref, ret_ref, q_ref, g_ref, prev_ref, kv_ref, far_ref, *refs):
     if h > 0:
         refs = refs[2:]
@@ -80,14 +76,16 @@
     qh = q_ref.reshape(ROWS, HD)
     gh = g_ref.reshape(ROWS, HD)
 
-    def each(body, first, stop, carry, width=2):
-        whole = (stop - first) // width
-
-        def wide(m, c):
-            return body(first + m * width, width, c)
-
-        carry = lax.fori_loop(0, whole, wide, carry)
-        return lax.fori_loop(first + whole * width, stop, lambda n, c: body(n, 1, c), carry)
+    def each(body, first, stop, carry):
+        for size in (4, 2, 1):
+            whole = (stop - first) // size
+
+            def wide(m, c, first=first, size=size):
+                return body(first + m * size, size, c)
+
+            carry = lax.fori_loop(0, whole, wide, carry)
+            first = first + whole * size
+        return carry
 
     def rows_at(n, width):
         return pl.ds(pl.multiple_of(n * BLOCK, BLOCK), width * BLOCK)
@@ -97,7 +95,7 @@
 
     def products(n, width):
         dp_ref[rows_at(n, width), :] = contract(blocks(n, width, 1), gh[...], ((1,), (1,)))
-        return contract(blocks(n, width, 0), qh[...], ((1,), (1,)))
+        return contract(blocks(n, width, 0), qh[...], ((1,), (1,))) * (SCALE * LOG2E)
 
     def score(n, width, top):
         s = products(n, width)
@@ -115,7 +113,7 @@
         return pl.ds(pl.multiple_of(n * BLOCK, BLOCK) + k * SLAB, SLAB)
 
     def weigh_one(n, total):
-        e = weigh(s_ref[rows_at(n, 1), :], top)
+        e = jnp.exp2(s_ref[rows_at(n, 1), :] - top)
         s_ref[rows_at(n, 1), :] = e
         return total + fold(e, jnp.add)
 
@@ -146,8 +144,8 @@
 
     each(grads, 0, count, 0)
     for g in range(GROUP):
-        piece = dqt[:, g * BLOCK:(g + 1) * BLOCK] * SCALE
-        dq_ref[g] = piece.T.astype(jnp.bfloat16)
+        piece = (dqt[:, g * BLOCK:(g + 1) * BLOCK] * SCALE).astype(jnp.bfloat16)
+        dq_ref[g] = piece.T
 
     @pl.when(b == per_device - 1)
     def _():
@@ -197,6 +195,25 @@
     )(own, window, retrieved, queries, output_grad, prev, kv, far, *carried)
 
 
+def wants_kernel(per_device, ret_ref, out_ref):
+    owners = lax.broadcasted_iota(jnp.int32, out_ref.shape, 0)
+    wants = jnp.full(out_ref.shape, -1, jnp.int32)
+    for b in range(per_device):
+        for r in range(MEMORY):
+            e = ret_ref[b, r]
+            wants = jnp.where(owners == e // per_device, jnp.maximum(wants, e % per_device), wants)
+    out_ref[...] = wants
+
+
+def wants_of(retrieved, shards):
+    return pl.pallas_call(
+        functools.partial(wants_kernel, retrieved.shape[0]),
+        in_specs=[pl.BlockSpec(memory_space=pltpu.SMEM)],
+        out_shape=jax.ShapeDtypeStruct((shards, 8, HD), jnp.int32),
+        name="wants",
+    )(retrieved)
+
+
 def exchange(array):
     return lax.all_to_all(array, "seq", split_axis=0, concat_axis=0, tiled=True)
 
@@ -212,10 +229,7 @@
     per_device = tokens // BLOCK
     shards = lax.axis_size("seq")
     own_index = lax.axis_index("seq").astype(jnp.int32).reshape(1)
-    named = retrieved.reshape(1, per_device * MEMORY)
-    owners = jnp.arange(shards, dtype=jnp.int32)[:, None]
-    wants = jnp.max(jnp.where(named // per_device == owners, named % per_device, -1), axis=1)
-    wanted = exchange(wants)
+    wanted = exchange(wants_of(retrieved, shards))[:, 0, 0]
 
     kv = jnp.stack([key_heads, value_heads]).reshape(2, per_device, BLOCK, KVH, HD)
     kv = kv.transpose(3, 1, 0, 2, 4)

time: 134 us -> 131 us (0.978)
  other arithmetic: 2.09 us -> 0.58 us
    pallas_call x0 -> x1, Pallas kernels: none -> 1.38 us  [wants_of(): pl.pallas_call(functools.partial(wants_kernel, retrieved.shape[0]), in_sp...]
where the time goes in v3:
time: 131 us; the launch traced here: 129 us
  waiting for transfers between devices  41.4 us (32%)
  starting transfers between devices  33.6 us (26%)
  blocking collectives  22.1 us (17%)
  Pallas kernels  21.8 us (17%)
  local copies, waits for them, and re-layouts  8.12 us (6%)
    ppermute x3, waiting for transfers between devices, shifted(): return lax.ppermute(array, 'seq', pairs)  25 us
    all_to_all x4, starting transfers between devices, exchange(): return lax.all_to_all(array, 'seq', split_axis=0, concat_axis=0, tiled=True)  24.4 us
    all_to_all x1, blocking collectives, exchange(): return lax.all_to_all(array, 'seq', split_axis=0, concat_axis=0, tiled=True)  22.1 us
    pallas_call x2, Pallas kernels, attention_grads(): pl.pallas_call(functools.partial(kernel, per_device, shards, h), grid=(pe...  20.4 us
    all_to_all x4, waiting for transfers between devices, exchange(): return lax.all_to_all(array, 'seq', split_axis=0, concat_axis=0, tiled=True)  16.4 us
    ppermute x3, starting transfers between devices, shifted(): return lax.ppermute(array, 'seq', pairs)  9.19 us
    unnamed x18, local copies, waits for them, and re-layouts  5.24 us
    gather x2, local copies, waits for them, and re-layouts, body(): outgoing = jnp.take(kv[h], jnp.maximum(wanted, 0), axis=0, mode='clip')  2.82 us
  transfers between devices with their start and end apart: 7, of which 6 were waited for; matrix products, arithmetic and copies ran while one was open for 3% of the time, Pallas kernels for 8%

profile of v3, /device:TPU:14, one launch (start us, length us, event | category | flops | bytes accessed | tf_op | source)
XLA Modules:
  0.0 129.1 jit_solution(5183717368787387370)
XLA Ops:
  0.6 1.4 %wants.1 = s32[8,8,128]{2,1,0:T(8,128)} custom-call(s32[3,4]{1,0:T(4,128)} %ret_ref.5), custom_call_target="tpu_custom_call" | custom-call | tf_op jit(solution)/shard_map/wants/pallas_call | solution.py:209
  2.0 6.2 %all-to-all-start = ((s32[8,8,128]{2,1,0:T(8,128)}), s32[8,8,128]{2,1,0:T(8,128)S(1)}, u32[]{:S(2)}, u32[]{:S(2)}) async-start(s32[8,8,128]{2,1,0:T(8,128)} %wants.1), calls=%async_computation | async-start | bytes 65536 | tf_op jit(solution)/shard_map/all_to_all | solution.py:218
  8.2 1.0 copy.19
  9.2 1.0 copy.20
  10.2 2.4 %all-to-all-done = s32[8,8,128]{2,1,0:T(8,128)S(1)} async-done(((s32[8,8,128]{2,1,0:T(8,128)}), s32[8,8,128]{2,1,0:T(8,128)S(1)}, u32[]{:S(2)}, u32[]{:S(2)}) %all-to-all-start) | async-done | bytes 32800 | tf_op jit(solution)/shard_map/all_to_all | solution.py:218
  13.0 1.4 %gather_fusion.1 = bf16[8,2,128,128]{3,2,1,0:T(8,128)(2,1)} fusion(bf16[3,2,128,128]{3,2,1,0:T(8,128)(2,1)S(1)} %get-tuple-element.31, s32[1024]{0:T(1024)S(1)} %pad_clamp_fusion), kind=kCustom, calls=%fused_computation.1 | custom fusion | bytes 1048608 | tf_op jit(solution)/shard_map/jit(_take)/gather | solution.py:245
  14.4 5.7 %all-to-all-start.2 = ((bf16[8,2,128,128]{3,2,1,0:T(8,128)(2,1)}), bf16[8,2,128,128]{3,2,1,0:T(8,128)(2,1)S(1)}, u32[]{:S(2)}, u32[]{:S(2)}) async-start(bf16[8,2,128,128]{3,2,1,0:T(8,128)(2,1)} %gather_fusion.1), calls=%async_computation.2 | async-start | bytes 1048576 | tf_op jit(solution)/shard_map/all_to_all | solution.py:218
  20.1 1.4 %gather_fusion = bf16[8,2,128,128]{3,2,1,0:T(8,128)(2,1)} fusion(bf16[3,2,128,128]{3,2,1,0:T(8,128)(2,1)S(1)} %get-tuple-element.32, s32[1024]{0:T(1024)S(1)} %pad_clamp_fusion), kind=kCustom, calls=%fused_computation | custom fusion | bytes 1048608 | tf_op jit(solution)/shard_map/jit(_take)/gather | solution.py:245
  21.5 9.1 %all-to-all-done.2.far_ref = bf16[8,2,128,128]{3,2,1,0:T(8,128)(2,1)S(1)} async-done(((bf16[8,2,128,128]{3,2,1,0:T(8,128)(2,1)}), bf16[8,2,128,128]{3,2,1,0:T(8,128)(2,1)S(1)}, u32[]{:S(2)}, u32[]{:S(2)}) %all-to-all-start.2) | async-done | bytes 524320 | tf_op jit(solution)/shard_map/all_to_all | solution.py:218
  30.6 6.5 %all-to-all-start.1 = ((bf16[8,2,128,128]{3,2,1,0:T(8,128)(2,1)}), bf16[8,2,128,128]{3,2,1,0:T(8,128)(2,1)S(1)}, u32[]{:S(2)}, u32[]{:S(2)}) async-start(bf16[8,2,128,128]{3,2,1,0:T(8,128)(2,1)} %gather_fusion), calls=%async_computation.1 | async-start | bytes 1048576 | tf_op jit(solution)/shard_map/all_to_all | solution.py:218
  37.1 3.4 %collective-permute-start = (bf16[2,3,2,128,128]{4,3,2,1,0:T(8,128)(2,1)S(1)}, bf16[2,3,2,128,128]{4,3,2,1,0:T(8,128)(2,1)S(1)}, u32[]{:S(2)}, u32[]{:S(2)}) collective-permute-start(bf16[2,3,2,128,128]{4,3,2,1,0:T(8,128)(2,1)S(1)} %maximum_bitcast_fusion.kv_ref), channel_id=1, source_target_pairs={{0,1},{1,2},{2,3},{3,4},{4,5},{5,6},{6,7},{8,9},{9,10},{10,11},{11... | collective-permute-start | bytes 1179656 | tf_op jit(solution)/shard_map/ppermute | solution.py:224
  40.5 15.5 %collective-permute-done.prev_ref = bf16[2,3,2,128,128]{4,3,2,1,0:T(8,128)(2,1)S(1)} collective-permute-done((bf16[2,3,2,128,128]{4,3,2,1,0:T(8,128)(2,1)S(1)}, bf16[2,3,2,128,128]{4,3,2,1,0:T(8,128)(2,1)S(1)}, u32[]{:S(2)}, u32[]{:S(2)}) %collective-permute-start) | collective-permute-done | bytes 393248 | tf_op jit(solution)/shard_map/ppermute | solution.py:224
  56.8 10.2 %shard_map.85 = (bf16[14,384,128]{2,1,0:T(8,128)(2,1)}, f32[2,3,2,128,128]{4,3,2,1,0:T(8,128)}, bf16[3,2,128,128]{3,2,1,0:T(8,128)(2,1)}, bf16[8,2,128,128]{3,2,1,0:T(8,128)(2,1)}) custom-call(s32[1]{0:T(128)} %bitcast.own_ref, s32[3]{0:T(128)} %win_ref.3, s32[3,4]{1,0:T(4,128)} %ret_ref.5, bf16[14,384,128]{2,1,0:T(8,128)(2,1)} %bitcast.46, ...), custom_call_target="tpu_custom_call" | custom-call | flops 3523215360 | bytes 5505024 | tf_op jit(solution)/shard_map/pallas_call | solution.py:169
  67.0 0.8 copy-done.3
  67.8 10.2 %shard_map.86 = (bf16[14,384,128]{2,1,0:T(8,128)(2,1)}, f32[2,3,2,128,128]{4,3,2,1,0:T(8,128)}, bf16[3,2,128,128]{3,2,1,0:T(8,128)(2,1)}, bf16[8,2,128,128]{3,2,1,0:T(8,128)(2,1)}) custom-call(s32[1]{0:T(128)} %bitcast.own_ref, s32[3]{0:T(128)} %win_ref.3, s32[3,4]{1,0:T(4,128)} %ret_ref.5, ...), custom_call_target="tpu_custom_call", output_to_operand_aliasing={{0}: (8, {}), {1}: (9, {})} | custom-call | flops 3523215360 | bytes 5505024 | tf_op jit(solution)/shard_map/pallas_call | solution.py:169
  78.0 22.1 %all_to_all.25 = bf16[8,2,128,128]{3,2,1,0:T(8,128)(2,1)S(1)} all-to-all(bf16[8,2,128,128]{3,2,1,0:T(8,128)(2,1)} %get-tuple-element.18), channel_id=1, replica_groups=mesh['dp'=4,'seq'=8] {'seq'}, dimensions={0} | all-to-all | bytes 1048576 | tf_op jit(solution)/shard_map/all_to_all | solution.py:218
  100.1 5.9 %all-to-all-start.3 = ((bf16[8,2,128,128]{3,2,1,0:T(8,128)(2,1)}), bf16[8,2,128,128]{3,2,1,0:T(8,128)(2,1)S(1)}, u32[]{:S(2)}, u32[]{:S(2)}) async-start(bf16[8,2,128,128]{3,2,1,0:T(8,128)(2,1)} %get-tuple-element.16), calls=%async_computation.3 | async-start | bytes 1048576 | tf_op jit(solution)/shard_map/all_to_all | solution.py:218
  106.1 2.5 %collective-permute-start.2 = (bf16[3,2,128,128]{3,2,1,0:T(8,128)(2,1)S(1)}, bf16[3,2,128,128]{3,2,1,0:T(8,128)(2,1)S(1)}, u32[]{:S(2)}, u32[]{:S(2)}) collective-permute-start(bf16[3,2,128,128]{3,2,1,0:T(8,128)(2,1)S(1)} %copy-done.6), channel_id=1, source_target_pairs={{1,0},{2,1},{3,2},{4,3},{5,4},{6,5},{7,6},{9,8},{10,9},{11,10},{12... | collective-permute-start | bytes 589832 | tf_op jit(solution)/shard_map/ppermute | solution.py:224
  108.5 3.4 %collective-permute-start.1 = (bf16[3,2,128,128]{3,2,1,0:T(8,128)(2,1)S(1)}, bf16[3,2,128,128]{3,2,1,0:T(8,128)(2,1)S(1)}, u32[]{:S(2)}, u32[]{:S(2)}) collective-permute-start(bf16[3,2,128,128]{3,2,1,0:T(8,128)(2,1)S(1)} %copy-done.5), channel_id=1, source_target_pairs={{1,0},{2,1},{3,2},{4,3},{5,4},{6,5},{7,6},{9,8},{10,9},{11,10},{12... | collective-permute-start | bytes 589832 | tf_op jit(solution)/shard_map/ppermute | solution.py:224
  112.3 4.9 %all-to-all-done.3 = bf16[8,2,128,128]{3,2,1,0:T(8,128)(2,1)S(1)} async-done(((bf16[8,2,128,128]{3,2,1,0:T(8,128)(2,1)}), bf16[8,2,128,128]{3,2,1,0:T(8,128)(2,1)S(1)}, u32[]{:S(2)}, u32[]{:S(2)}) %all-to-all-start.3) | async-done | bytes 524320 | tf_op jit(solution)/shard_map/all_to_all | solution.py:218
  117.6 7.0 %collective-permute-done.2 = bf16[3,2,128,128]{3,2,1,0:T(8,128)(2,1)S(1)} collective-permute-done((bf16[3,2,128,128]{3,2,1,0:T(8,128)(2,1)S(1)}, bf16[3,2,128,128]{3,2,1,0:T(8,128)(2,1)S(1)}, u32[]{:S(2)}, u32[]{:S(2)}) %collective-permute-start.2) | collective-permute-done | bytes 196640 | tf_op jit(solution)/shard_map/ppermute | solution.py:224
  124.6 2.5 %collective-permute-done.1 = bf16[3,2,128,128]{3,2,1,0:T(8,128)(2,1)S(1)} collective-permute-done((bf16[3,2,128,128]{3,2,1,0:T(8,128)(2,1)S(1)}, bf16[3,2,128,128]{3,2,1,0:T(8,128)(2,1)S(1)}, u32[]{:S(2)}, u32[]{:S(2)}) %collective-permute-start.1) | collective-permute-done | bytes 196640 | tf_op jit(solution)/shard_map/ppermute | solution.py:224
  127.4 0.9 copy.26
  128.2 0.9 copy.25
  (23 shorter events, 2.2 us)
Async XLA Ops:
  2.0 10.6 %all-to-all-start = ((s32[8,8,128]{2,1,0:T(8,128)}), s32[8,8,128]{2,1,0:T(8,128)S(1)}, u32[]{:S(2)}, u32[]{:S(2)}) async-start(s32[8,8,128]{2,1,0:T(8,128)} %wants.1), calls=%async_computation | async-start | bytes 65536 | tf_op jit(solution)/shard_map/all_to_all | solution.py:218
  10.2 26.9 %copy-start = (bf16[2,3,2,128,128]{4,3,2,1,0:T(8,128)(2,1)}, bf16[2,3,2,128,128]{4,3,2,1,0:T(8,128)(2,1)S(1)}, u32[]{:S(2)}) copy-start(bf16[2,3,2,128,128]{4,3,2,1,0:T(8,128)(2,1)S(1)} %maximum_bitcast_fusion.kv_ref) | copy-start | bytes 1179652
  14.4 16.2 %all-to-all-start.2 = ((bf16[8,2,128,128]{3,2,1,0:T(8,128)(2,1)}), bf16[8,2,128,128]{3,2,1,0:T(8,128)(2,1)S(1)}, u32[]{:S(2)}, u32[]{:S(2)}) async-start(bf16[8,2,128,128]{3,2,1,0:T(8,128)(2,1)} %gather_fusion.1), calls=%async_computation.2 | async-start | bytes 1048576 | tf_op jit(solution)/shard_map/all_to_all | solution.py:218
  30.6 25.4 %copy-start.2 = (bf16[8,2,128,128]{3,2,1,0:T(8,128)(2,1)}, bf16[8,2,128,128]{3,2,1,0:T(8,128)(2,1)S(1)}, u32[]{:S(2)}) copy-start(bf16[8,2,128,128]{3,2,1,0:T(8,128)(2,1)S(1)} %all-to-all-done.2.far_ref) | copy-start | bytes 1572868
  30.6 36.4 %all-to-all-start.1 = ((bf16[8,2,128,128]{3,2,1,0:T(8,128)(2,1)}), bf16[8,2,128,128]{3,2,1,0:T(8,128)(2,1)S(1)}, u32[]{:S(2)}, u32[]{:S(2)}) async-start(bf16[8,2,128,128]{3,2,1,0:T(8,128)(2,1)} %gather_fusion), calls=%async_computation.1 | async-start | bytes 1048576 | tf_op jit(solution)/shard_map/all_to_all | solution.py:218
  37.1 18.9 %collective-permute-start = (bf16[2,3,2,128,128]{4,3,2,1,0:T(8,128)(2,1)S(1)}, bf16[2,3,2,128,128]{4,3,2,1,0:T(8,128)(2,1)S(1)}, u32[]{:S(2)}, u32[]{:S(2)}) collective-permute-start(bf16[2,3,2,128,128]{4,3,2,1,0:T(8,128)(2,1)S(1)} %maximum_bitcast_fusion.kv_ref), channel_id=1, source_target_pairs={{0,1},{1,2},{2,3},{3,4},{4,5},{5,6},{6,7},{8,9},{9,10},{10,11},{11... | collective-permute-start | bytes 1179656 | tf_op jit(solution)/shard_map/ppermute | solution.py:224
  56.0 0.8 copy-start.4
  67.0 0.8 copy-start.3
  78.0 28.0 %copy-start.6 = (bf16[3,2,128,128]{3,2,1,0:T(8,128)(2,1)S(1)}, bf16[3,2,128,128]{3,2,1,0:T(8,128)(2,1)}, u32[]{:S(2)}) copy-start(bf16[3,2,128,128]{3,2,1,0:T(8,128)(2,1)} %get-tuple-element.17) | copy-start | bytes 589828
  78.0 30.5 %copy-start.5 = (bf16[3,2,128,128]{3,2,1,0:T(8,128)(2,1)S(1)}, bf16[3,2,128,128]{3,2,1,0:T(8,128)(2,1)}, u32[]{:S(2)}) copy-start(bf16[3,2,128,128]{3,2,1,0:T(8,128)(2,1)} %get-tuple-element.15) | copy-start | bytes 589828
  100.1 27.0 %copy-start.1 = (f32[2,3,2,128,128]{4,3,2,1,0:T(8,128)S(1)}, f32[2,3,2,128,128]{4,3,2,1,0:T(8,128)}, u32[]{:S(2)}) copy-start(f32[2,3,2,128,128]{4,3,2,1,0:T(8,128)} %get-tuple-element.14) | copy-start | bytes 2359300
  100.1 17.1 %all-to-all-start.3 = ((bf16[8,2,128,128]{3,2,1,0:T(8,128)(2,1)}), bf16[8,2,128,128]{3,2,1,0:T(8,128)(2,1)S(1)}, u32[]{:S(2)}, u32[]{:S(2)}) async-start(bf16[8,2,128,128]{3,2,1,0:T(8,128)(2,1)} %get-tuple-element.16), calls=%async_computation.3 | async-start | bytes 1048576 | tf_op jit(solution)/shard_map/all_to_all | solution.py:218
  106.1 18.6 %collective-permute-start.2 = (bf16[3,2,128,128]{3,2,1,0:T(8,128)(2,1)S(1)}, bf16[3,2,128,128]{3,2,1,0:T(8,128)(2,1)S(1)}, u32[]{:S(2)}, u32[]{:S(2)}) collective-permute-start(bf16[3,2,128,128]{3,2,1,0:T(8,128)(2,1)S(1)} %copy-done.6), channel_id=1, source_target_pairs={{1,0},{2,1},{3,2},{4,3},{5,4},{6,5},{7,6},{9,8},{10,9},{11,10},{12... | collective-permute-start | bytes 589832 | tf_op jit(solution)/shard_map/ppermute | solution.py:224
  108.5 18.6 %collective-permute-start.1 = (bf16[3,2,128,128]{3,2,1,0:T(8,128)(2,1)S(1)}, bf16[3,2,128,128]{3,2,1,0:T(8,128)(2,1)S(1)}, u32[]{:S(2)}, u32[]{:S(2)}) collective-permute-start(bf16[3,2,128,128]{3,2,1,0:T(8,128)(2,1)S(1)} %copy-done.5), channel_id=1, source_target_pairs={{1,0},{2,1},{3,2},{4,3},{5,4},{6,5},{7,6},{9,8},{10,9},{11,10},{12... | collective-permute-start | bytes 589832 | tf_op jit(solution)/shard_map/ppermute | solution.py:224

commit v4 on v3

--- a/solution.py
+++ b/solution.py
@@ -97,16 +97,20 @@
         dp_ref[rows_at(n, width), :] = contract(blocks(n, width, 1), gh[...], ((1,), (1,)))
         return contract(blocks(n, width, 0), qh[...], ((1,), (1,))) * (SCALE * LOG2E)
 
+    key_pos = lax.broadcasted_iota(jnp.int32, (BLOCK, BLOCK), 0)
+    query_pos = lax.broadcasted_iota(jnp.int32, (BLOCK, BLOCK), 1)
+    above = jnp.where(key_pos <= query_pos, 0, 1)
+
     def score(n, width, top):
         s = products(n, width)
+        hidden = above > n
+        own = jnp.concatenate(
+            [jnp.where(hidden, masked_score, s[:BLOCK, g * BLOCK:(g + 1) * BLOCK]) for g in range(GROUP)], axis=1)
+        s = own if width == 1 else jnp.concatenate([own, s[BLOCK:]], axis=0)
         s_ref[rows_at(n, width), :] = s
         return jnp.maximum(top, fold(s, jnp.maximum))
 
-    key_pos = lax.broadcasted_iota(jnp.int32, (BLOCK, ROWS), 0)
-    query_pos = lax.broadcasted_iota(jnp.int32, (BLOCK, ROWS), 1) % BLOCK
-    s = jnp.where(key_pos <= query_pos, products(0, 1), masked_score)
-    s_ref[rows_at(0, 1), :] = s
-    top = each(score, 1, count, fold(s, jnp.maximum))
+    top = each(score, 0, count, jnp.full((8, ROWS), masked_score, jnp.float32))
     top = jnp.max(top, axis=0, keepdims=True)
 
     def slab(n, k):
@@ -173,10 +177,10 @@
         + [pl.BlockSpec(memory_space=pl.ANY)] * len(carried),
         out_specs=[tokens, of_head, pl.BlockSpec((per_device, *pair), lambda b: (0, 0, 0, 0)), of_owner],
         out_shape=[
-            jax.ShapeDtypeStruct(queries.shape, jnp.bfloat16),
-            jax.ShapeDtypeStruct((KVH, per_device, *pair), jnp.float32),
-            jax.ShapeDtypeStruct((per_device, *pair), jnp.bfloat16),
-            jax.ShapeDtypeStruct((shards, *pair), jnp.bfloat16),
+            pltpu.HBM(queries.shape, jnp.bfloat16),
+            pltpu.HBM((KVH, per_device, *pair), jnp.float32),
+            pltpu.HBM((per_device, *pair), jnp.bfloat16),
+            pltpu.HBM((shards, *pair), jnp.bfloat16),
         ],
         scratch_shapes=[
             pltpu.VMEM((total, *pair), jnp.bfloat16),
@@ -192,6 +196,7 @@
             transcendentals=per_device * most * BLOCK * ROWS,
             bytes_accessed=8 * queries.size,
         ),
+        compiler_params=pltpu.CompilerParams(vmem_limit_bytes=36 << 20),
     )(own, window, retrieved, queries, output_grad, prev, kv, far, *carried)
 
 
@@ -235,8 +240,8 @@
     kv = kv.transpose(3, 1, 0, 2, 4)
     prev = shifted(kv, 1)
     slot_hits = (wanted[:, None] == jnp.arange(per_device)[None, :]).astype(jnp.bfloat16)
-    queries = queries.transpose(1, 0, 2)
-    output_grad = output_grad.transpose(1, 0, 2)
+    queries = pltpu.with_memory_space_constraint(queries.transpose(1, 0, 2), pltpu.HBM)
+    output_grad = pltpu.with_memory_space_constraint(output_grad.transpose(1, 0, 2), pltpu.HBM)
     carried = ()
     fars = []
     replies = []

time: 131 us -> 129 us (0.985)
  the two profiles are of different devices: /device:TPU:14 before, /device:TPU:10 now
where the time goes in v4:
time: 129 us
  waiting for transfers between devices  42.1 us (33%)
  starting transfers between devices  34.5 us (27%)
  Pallas kernels  24.3 us (19%)
  blocking collectives  19 us (15%)
  local copies, waits for them, and re-layouts  6.58 us (5%)
    ppermute x3, waiting for transfers between devices, shifted(): return lax.ppermute(array, 'seq', pairs)  25.3 us
    all_to_all x4, starting transfers between devices, exchange(): return lax.all_to_all(array, 'seq', split_axis=0, concat_axis=0, tiled=True)  25.3 us
    pallas_call x2, Pallas kernels, attention_grads(): pl.pallas_call(functools.partial(kernel, per_device, shards, h), grid=(pe...  22.9 us
    all_to_all x1, blocking collectives, exchange(): return lax.all_to_all(array, 'seq', split_axis=0, concat_axis=0, tiled=True)  19 us
    all_to_all x4, waiting for transfers between devices, exchange(): return lax.all_to_all(array, 'seq', split_axis=0, concat_axis=0, tiled=True)  16.7 us
    ppermute x3, starting transfers between devices, shifted(): return lax.ppermute(array, 'seq', pairs)  9.19 us
    unnamed x14, local copies, waits for them, and re-layouts  3.69 us
    gather x2, local copies, waits for them, and re-layouts, body(): outgoing = jnp.take(kv[h], jnp.maximum(wanted, 0), axis=0, mode='clip')  2.83 us
  transfers between devices with their start and end apart: 7, of which 6 were waited for; matrix products, arithmetic and copies ran while one was open for 3% of the time, Pallas kernels for 9%

profile of v4, /device:TPU:10, one launch (start us, length us, event | category | flops | bytes accessed | tf_op | source)
XLA Modules:
  0.0 128.6 jit_solution(5900690162016448682)
XLA Ops:
  0.6 1.4 %wants.1 = s32[8,8,128]{2,1,0:T(8,128)} custom-call(s32[3,4]{1,0:T(4,128)} %ret_ref.5), custom_call_target="tpu_custom_call" | custom-call | tf_op jit(solution)/shard_map/wants/pallas_call | solution.py:214
  2.0 6.2 %all-to-all-start = ((s32[8,8,128]{2,1,0:T(8,128)}), s32[8,8,128]{2,1,0:T(8,128)S(1)}, u32[]{:S(2)}, u32[]{:S(2)}) async-start(s32[8,8,128]{2,1,0:T(8,128)} %wants.1), calls=%async_computation | async-start | bytes 65536 | tf_op jit(solution)/shard_map/all_to_all | solution.py:223
  8.2 1.0 copy.19
  9.2 1.0 copy.20
  10.2 2.4 %all-to-all-done = s32[8,8,128]{2,1,0:T(8,128)S(1)} async-done(((s32[8,8,128]{2,1,0:T(8,128)}), s32[8,8,128]{2,1,0:T(8,128)S(1)}, u32[]{:S(2)}, u32[]{:S(2)}) %all-to-all-start) | async-done | bytes 32800 | tf_op jit(solution)/shard_map/all_to_all | solution.py:223
  13.0 1.4 %gather_fusion.1 = bf16[8,2,128,128]{3,2,1,0:T(8,128)(2,1)} fusion(bf16[3,2,128,128]{3,2,1,0:T(8,128)(2,1)S(1)} %get-tuple-element.31, s32[1024]{0:T(1024)S(1)} %pad_clamp_fusion), kind=kCustom, calls=%fused_computation.1 | custom fusion | bytes 1048608 | tf_op jit(solution)/shard_map/jit(_take)/gather | solution.py:250
  14.4 5.9 %all-to-all-start.2 = ((bf16[8,2,128,128]{3,2,1,0:T(8,128)(2,1)}), bf16[8,2,128,128]{3,2,1,0:T(8,128)(2,1)S(1)}, u32[]{:S(2)}, u32[]{:S(2)}) async-start(bf16[8,2,128,128]{3,2,1,0:T(8,128)(2,1)} %gather_fusion.1), calls=%async_computation.2 | async-start | bytes 1048576 | tf_op jit(solution)/shard_map/all_to_all | solution.py:223
  20.3 1.4 %gather_fusion = bf16[8,2,128,128]{3,2,1,0:T(8,128)(2,1)} fusion(bf16[3,2,128,128]{3,2,1,0:T(8,128)(2,1)S(1)} %get-tuple-element.32, s32[1024]{0:T(1024)S(1)} %pad_clamp_fusion), kind=kCustom, calls=%fused_computation | custom fusion | bytes 1048608 | tf_op jit(solution)/shard_map/jit(_take)/gather | solution.py:250
  21.7 9.1 %all-to-all-done.2.far_ref = bf16[8,2,128,128]{3,2,1,0:T(8,128)(2,1)S(1)} async-done(((bf16[8,2,128,128]{3,2,1,0:T(8,128)(2,1)}), bf16[8,2,128,128]{3,2,1,0:T(8,128)(2,1)S(1)}, u32[]{:S(2)}, u32[]{:S(2)}) %all-to-all-start.2) | async-done | bytes 524320 | tf_op jit(solution)/shard_map/all_to_all | solution.py:223
  30.8 6.5 %all-to-all-start.1 = ((bf16[8,2,128,128]{3,2,1,0:T(8,128)(2,1)}), bf16[8,2,128,128]{3,2,1,0:T(8,128)(2,1)S(1)}, u32[]{:S(2)}, u32[]{:S(2)}) async-start(bf16[8,2,128,128]{3,2,1,0:T(8,128)(2,1)} %gather_fusion), calls=%async_computation.1 | async-start | bytes 1048576 | tf_op jit(solution)/shard_map/all_to_all | solution.py:223
  37.3 3.4 %collective-permute-start = (bf16[2,3,2,128,128]{4,3,2,1,0:T(8,128)(2,1)S(1)}, bf16[2,3,2,128,128]{4,3,2,1,0:T(8,128)(2,1)S(1)}, u32[]{:S(2)}, u32[]{:S(2)}) collective-permute-start(bf16[2,3,2,128,128]{4,3,2,1,0:T(8,128)(2,1)S(1)} %maximum_bitcast_fusion.kv_ref), channel_id=1, source_target_pairs={{0,1},{1,2},{2,3},{3,4},{4,5},{5,6},{6,7},{8,9},{9,10},{10,11},{11... | collective-permute-start | bytes 1179656 | tf_op jit(solution)/shard_map/ppermute | solution.py:229
  40.7 15.5 %collective-permute-done.prev_ref = bf16[2,3,2,128,128]{4,3,2,1,0:T(8,128)(2,1)S(1)} collective-permute-done((bf16[2,3,2,128,128]{4,3,2,1,0:T(8,128)(2,1)S(1)}, bf16[2,3,2,128,128]{4,3,2,1,0:T(8,128)(2,1)S(1)}, u32[]{:S(2)}, u32[]{:S(2)}) %collective-permute-start) | collective-permute-done | bytes 393248 | tf_op jit(solution)/shard_map/ppermute | solution.py:229
  56.2 11.4 %shard_map.85 = (bf16[14,384,128]{2,1,0:T(8,128)(2,1)}, f32[2,3,2,128,128]{4,3,2,1,0:T(8,128)}, bf16[3,2,128,128]{3,2,1,0:T(8,128)(2,1)}, bf16[8,2,128,128]{3,2,1,0:T(8,128)(2,1)}) custom-call(s32[1]{0:T(128)} %bitcast.own_ref, s32[3]{0:T(128)S(1)} %copy-done.1, s32[3,4]{1,0:T(4,128)S(1)} %copy-done, bf16[14,384,128]{2,1,0:T(8,128)(2,1)} %bitcast.46, ...), custom_call_target="tpu_custom_call" | custom-call | flops 3523215360 | bytes 5505024 | tf_op jit(solution)/shard_map/pallas_call | solution.py:173
  67.6 11.4 %shard_map.86 = (bf16[14,384,128]{2,1,0:T(8,128)(2,1)}, f32[2,3,2,128,128]{4,3,2,1,0:T(8,128)}, bf16[3,2,128,128]{3,2,1,0:T(8,128)(2,1)}, bf16[8,2,128,128]{3,2,1,0:T(8,128)(2,1)}) custom-call(s32[1]{0:T(128)} %bitcast.own_ref, s32[3]{0:T(128)S(1)} %copy-done.1, s32[3,4]{1,0:T(4,128)S(1)} %copy-done, ...), custom_call_target="tpu_custom_call", output_to_operand_aliasing={{0}: (8, {}), {1}: (9, {})} | custom-call | flops 3523215360 | bytes 5505024 | tf_op jit(solution)/shard_map/pallas_call | solution.py:173
  79.1 19.0 %all_to_all.25 = bf16[8,2,128,128]{3,2,1,0:T(8,128)(2,1)S(1)} all-to-all(bf16[8,2,128,128]{3,2,1,0:T(8,128)(2,1)} %get-tuple-element.18), channel_id=1, replica_groups=mesh['dp'=4,'seq'=8] {'seq'}, dimensions={0} | all-to-all | bytes 1048576 | tf_op jit(solution)/shard_map/all_to_all | solution.py:223
  98.1 6.7 %all-to-all-start.3 = ((bf16[8,2,128,128]{3,2,1,0:T(8,128)(2,1)}), bf16[8,2,128,128]{3,2,1,0:T(8,128)(2,1)S(1)}, u32[]{:S(2)}, u32[]{:S(2)}) async-start(bf16[8,2,128,128]{3,2,1,0:T(8,128)(2,1)} %get-tuple-element.16), calls=%async_computation.3 | async-start | bytes 1048576 | tf_op jit(solution)/shard_map/all_to_all | solution.py:223
  104.8 2.5 %collective-permute-start.2 = (bf16[3,2,128,128]{3,2,1,0:T(8,128)(2,1)S(1)}, bf16[3,2,128,128]{3,2,1,0:T(8,128)(2,1)S(1)}, u32[]{:S(2)}, u32[]{:S(2)}) collective-permute-start(bf16[3,2,128,128]{3,2,1,0:T(8,128)(2,1)S(1)} %copy-done.4), channel_id=1, source_target_pairs={{1,0},{2,1},{3,2},{4,3},{5,4},{6,5},{7,6},{9,8},{10,9},{11,10},{12... | collective-permute-start | bytes 589832 | tf_op jit(solution)/shard_map/ppermute | solution.py:229
  107.3 3.4 %collective-permute-start.1 = (bf16[3,2,128,128]{3,2,1,0:T(8,128)(2,1)S(1)}, bf16[3,2,128,128]{3,2,1,0:T(8,128)(2,1)S(1)}, u32[]{:S(2)}, u32[]{:S(2)}) collective-permute-start(bf16[3,2,128,128]{3,2,1,0:T(8,128)(2,1)S(1)} %copy-done.3), channel_id=1, source_target_pairs={{1,0},{2,1},{3,2},{4,3},{5,4},{6,5},{7,6},{9,8},{10,9},{11,10},{12... | collective-permute-start | bytes 589832 | tf_op jit(solution)/shard_map/ppermute | solution.py:229
  110.6 0.4 fusion
  111.0 5.3 %all-to-all-done.3 = bf16[8,2,128,128]{3,2,1,0:T(8,128)(2,1)S(1)} async-done(((bf16[8,2,128,128]{3,2,1,0:T(8,128)(2,1)}), bf16[8,2,128,128]{3,2,1,0:T(8,128)(2,1)S(1)}, u32[]{:S(2)}, u32[]{:S(2)}) %all-to-all-start.3) | async-done | bytes 524320 | tf_op jit(solution)/shard_map/all_to_all | solution.py:223
  116.7 6.7 %collective-permute-done.2 = bf16[3,2,128,128]{3,2,1,0:T(8,128)(2,1)S(1)} collective-permute-done((bf16[3,2,128,128]{3,2,1,0:T(8,128)(2,1)S(1)}, bf16[3,2,128,128]{3,2,1,0:T(8,128)(2,1)S(1)}, u32[]{:S(2)}, u32[]{:S(2)}) %collective-permute-start.2) | collective-permute-done | bytes 196640 | tf_op jit(solution)/shard_map/ppermute | solution.py:229
  123.4 3.1 %collective-permute-done.1 = bf16[3,2,128,128]{3,2,1,0:T(8,128)(2,1)S(1)} collective-permute-done((bf16[3,2,128,128]{3,2,1,0:T(8,128)(2,1)S(1)}, bf16[3,2,128,128]{3,2,1,0:T(8,128)(2,1)S(1)}, u32[]{:S(2)}, u32[]{:S(2)}) %collective-permute-start.1) | collective-permute-done | bytes 196640 | tf_op jit(solution)/shard_map/ppermute | solution.py:229
  126.8 0.9 copy.26
  127.7 0.9 copy.25
  (19 shorter events, 1.1 us)
Async XLA Ops:
  2.0 10.6 %all-to-all-start = ((s32[8,8,128]{2,1,0:T(8,128)}), s32[8,8,128]{2,1,0:T(8,128)S(1)}, u32[]{:S(2)}, u32[]{:S(2)}) async-start(s32[8,8,128]{2,1,0:T(8,128)} %wants.1), calls=%async_computation | async-start | bytes 65536 | tf_op jit(solution)/shard_map/all_to_all | solution.py:223
  14.4 41.8 %copy-start = (s32[3,4]{1,0:T(4,128)S(1)}, s32[3,4]{1,0:T(4,128)}, u32[]{:S(2)}) copy-start(s32[3,4]{1,0:T(4,128)} %ret_ref.5) | copy-start | bytes 148
  14.4 41.8 %copy-start.1 = (s32[3]{0:T(128)S(1)}, s32[3]{0:T(128)}, u32[]{:S(2)}) copy-start(s32[3]{0:T(128)} %win_ref.3) | copy-start | bytes 40
  14.4 16.3 %all-to-all-start.2 = ((bf16[8,2,128,128]{3,2,1,0:T(8,128)(2,1)}), bf16[8,2,128,128]{3,2,1,0:T(8,128)(2,1)S(1)}, u32[]{:S(2)}, u32[]{:S(2)}) async-start(bf16[8,2,128,128]{3,2,1,0:T(8,128)(2,1)} %gather_fusion.1), calls=%async_computation.2 | async-start | bytes 1048576 | tf_op jit(solution)/shard_map/all_to_all | solution.py:223
  30.8 36.8 %all-to-all-start.1 = ((bf16[8,2,128,128]{3,2,1,0:T(8,128)(2,1)}), bf16[8,2,128,128]{3,2,1,0:T(8,128)(2,1)S(1)}, u32[]{:S(2)}, u32[]{:S(2)}) async-start(bf16[8,2,128,128]{3,2,1,0:T(8,128)(2,1)} %gather_fusion), calls=%async_computation.1 | async-start | bytes 1048576 | tf_op jit(solution)/shard_map/all_to_all | solution.py:223
  37.3 18.9 %collective-permute-start = (bf16[2,3,2,128,128]{4,3,2,1,0:T(8,128)(2,1)S(1)}, bf16[2,3,2,128,128]{4,3,2,1,0:T(8,128)(2,1)S(1)}, u32[]{:S(2)}, u32[]{:S(2)}) collective-permute-start(bf16[2,3,2,128,128]{4,3,2,1,0:T(8,128)(2,1)S(1)} %maximum_bitcast_fusion.kv_ref), channel_id=1, source_target_pairs={{0,1},{1,2},{2,3},{3,4},{4,5},{5,6},{6,7},{8,9},{9,10},{10,11},{11... | collective-permute-start | bytes 1179656 | tf_op jit(solution)/shard_map/ppermute | solution.py:229
  79.0 25.7 %copy-start.4 = (bf16[3,2,128,128]{3,2,1,0:T(8,128)(2,1)S(1)}, bf16[3,2,128,128]{3,2,1,0:T(8,128)(2,1)}, u32[]{:S(2)}) copy-start(bf16[3,2,128,128]{3,2,1,0:T(8,128)(2,1)} %get-tuple-element.17) | copy-start | bytes 589828
  79.1 28.2 %copy-start.3 = (bf16[3,2,128,128]{3,2,1,0:T(8,128)(2,1)S(1)}, bf16[3,2,128,128]{3,2,1,0:T(8,128)(2,1)}, u32[]{:S(2)}) copy-start(bf16[3,2,128,128]{3,2,1,0:T(8,128)(2,1)} %get-tuple-element.15) | copy-start | bytes 589828
  98.1 28.5 %copy-start.2 = (f32[2,3,2,128,128]{4,3,2,1,0:T(8,128)S(1)}, f32[2,3,2,128,128]{4,3,2,1,0:T(8,128)}, u32[]{:S(2)}) copy-start(f32[2,3,2,128,128]{4,3,2,1,0:T(8,128)} %get-tuple-element.14) | copy-start | bytes 2359300
  98.1 18.3 %all-to-all-start.3 = ((bf16[8,2,128,128]{3,2,1,0:T(8,128)(2,1)}), bf16[8,2,128,128]{3,2,1,0:T(8,128)(2,1)S(1)}, u32[]{:S(2)}, u32[]{:S(2)}) async-start(bf16[8,2,128,128]{3,2,1,0:T(8,128)(2,1)} %get-tuple-element.16), calls=%async_computation.3 | async-start | bytes 1048576 | tf_op jit(solution)/shard_map/all_to_all | solution.py:223
  104.8 18.7 %collective-permute-start.2 = (bf16[3,2,128,128]{3,2,1,0:T(8,128)(2,1)S(1)}, bf16[3,2,128,128]{3,2,1,0:T(8,128)(2,1)S(1)}, u32[]{:S(2)}, u32[]{:S(2)}) collective-permute-start(bf16[3,2,128,128]{3,2,1,0:T(8,128)(2,1)S(1)} %copy-done.4), channel_id=1, source_target_pairs={{1,0},{2,1},{3,2},{4,3},{5,4},{6,5},{7,6},{9,8},{10,9},{11,10},{12... | collective-permute-start | bytes 589832 | tf_op jit(solution)/shard_map/ppermute | solution.py:229
  107.3 19.3 %collective-permute-start.1 = (bf16[3,2,128,128]{3,2,1,0:T(8,128)(2,1)S(1)}, bf16[3,2,128,128]{3,2,1,0:T(8,128)(2,1)S(1)}, u32[]{:S(2)}, u32[]{:S(2)}) collective-permute-start(bf16[3,2,128,128]{3,2,1,0:T(8,128)(2,1)S(1)} %copy-done.3), channel_id=1, source_target_pairs={{1,0},{2,1},{3,2},{4,3},{5,4},{6,5},{7,6},{9,8},{10,9},{11,10},{12... | collective-permute-start | bytes 589832 | tf_op jit(solution)/shard_map/ppermute | solution.py:229

commit v5 on v4

--- a/solution.py
+++ b/solution.py
@@ -14,7 +14,7 @@
 KVH = 2
 GROUP = QH // KVH
 BLOCK = 128
-SLAB = 16
+SLAB = 32
 MEMORY = 4
 ROWS = GROUP * BLOCK
 SCALE = HD ** (-0.5)
@@ -67,7 +67,7 @@
     @pl.when(b == 0)
     def _():
         acc[...] = jnp.zeros_like(acc)
-        kvs[0:per_device] = prev_ref[0]
+        kvs[0:per_device] = prev_ref[...]
         kvs[per_device:near] = kv_ref[0]
         kvs[near:near + shards] = far_ref[...]
 
@@ -170,12 +170,13 @@
     tokens = pl.BlockSpec((GROUP, BLOCK, HD), lambda b: (h, b, 0))
     of_head = pl.BlockSpec((1, per_device, *pair), lambda b: (h, 0, 0, 0, 0))
     of_owner = pl.BlockSpec((shards, *pair), lambda b: (0, 0, 0, 0))
+    of_device = pl.BlockSpec((per_device, *pair), lambda b: (0, 0, 0, 0))
     return pl.pallas_call(
         functools.partial(kernel, per_device, shards, h),
         grid=(per_device,),
-        in_specs=[smem, smem, smem, tokens, tokens, of_head, of_head, of_owner]
+        in_specs=[smem, smem, smem, tokens, tokens, of_device, of_head, of_owner]
         + [pl.BlockSpec(memory_space=pl.ANY)] * len(carried),
-        out_specs=[tokens, of_head, pl.BlockSpec((per_device, *pair), lambda b: (0, 0, 0, 0)), of_owner],
+        out_specs=[tokens, of_head, of_device, of_owner],
         out_shape=[
             pltpu.HBM(queries.shape, jnp.bfloat16),
             pltpu.HBM((KVH, per_device, *pair), jnp.float32),
@@ -219,6 +220,24 @@
     )(retrieved)
 
 
+def pick_kernel(shards, wants_ref, kv_ref, out_ref):
+    for d in range(shards):
+        out_ref[d] = kv_ref[0, jnp.maximum(jnp.max(wants_ref[d]), 0)]
+
+
+def pick(h, wants, kv):
+    shards = wants.shape[0]
+    return pl.pallas_call(
+        functools.partial(pick_kernel, shards),
+        grid=(1,),
+        in_specs=[pl.BlockSpec(wants.shape, lambda i: (0, 0, 0)),
+                  pl.BlockSpec((1, *kv.shape[1:]), lambda i: (h, 0, 0, 0, 0))],
+        out_specs=pl.BlockSpec((shards, *kv.shape[2:]), lambda i: (0, 0, 0, 0)),
+        out_shape=pltpu.HBM((shards, *kv.shape[2:]), kv.dtype),
+        compiler_params=pltpu.CompilerParams(vmem_limit_bytes=16 << 20),
+    )(wants, kv)
+
+
 def exchange(array):
     return lax.all_to_all(array, "seq", split_axis=0, concat_axis=0, tiled=True)
 
@@ -234,11 +253,12 @@
     per_device = tokens // BLOCK
     shards = lax.axis_size("seq")
     own_index = lax.axis_index("seq").astype(jnp.int32).reshape(1)
-    wanted = exchange(wants_of(retrieved, shards))[:, 0, 0]
+    wants = exchange(wants_of(retrieved, shards))
+    wanted = wants[:, 0, 0]
 
     kv = jnp.stack([key_heads, value_heads]).reshape(2, per_device, BLOCK, KVH, HD)
     kv = kv.transpose(3, 1, 0, 2, 4)
-    prev = shifted(kv, 1)
+    prevs = [shifted(kv[h], 1) for h in range(KVH)]
     slot_hits = (wanted[:, None] == jnp.arange(per_device)[None, :]).astype(jnp.bfloat16)
     queries = pltpu.with_memory_space_constraint(queries.transpose(1, 0, 2), pltpu.HBM)
     output_grad = pltpu.with_memory_space_constraint(output_grad.transpose(1, 0, 2), pltpu.HBM)
@@ -247,11 +267,11 @@
     replies = []
     returned = []
     for h in range(KVH):
-        outgoing = jnp.take(kv[h], jnp.maximum(wanted, 0), axis=0, mode="clip")
+        outgoing = pick(h, wants, kv)
         fars.append(exchange(outgoing))
     for h in range(KVH):
         *carried, dprev, dfar = attention_grads(
-            h, own_index, window, retrieved, queries, output_grad, prev, kv, fars[h], *carried
+            h, own_index, window, retrieved, queries, output_grad, prevs[h], kv, fars[h], *carried
         )
         replies.append(exchange(dfar))
         returned.append(shifted(dprev, -1).astype(jnp.float32))

time: 129 us -> 123 us (0.953)
  waiting for transfers between devices: 42.1 us -> 34.9 us
  local copies, waits for them, and re-layouts: 6.58 us -> 3.98 us
  starting transfers between devices: 34.5 us -> 37 us
  Pallas kernels: 24.3 us -> 25.9 us
    ppermute x3 -> x4, waiting for transfers between devices: 25.3 us -> 18.3 us  [shifted(): return lax.ppermute(array, 'seq', pairs)]
    ppermute x3 -> x4, starting transfers between devices: 9.19 us -> 12.6 us  [shifted(): return lax.ppermute(array, 'seq', pairs)]
    gather x2 -> x0, local copies, waits for them, and re-layouts: 2.83 us -> none  [body(): outgoing = jnp.take(kv[h], jnp.maximum(wanted, 0), axis=0, mode='clip')]
    pallas_call x0 -> x2, Pallas kernels: none -> 2.04 us  [pick(): pl.pallas_call(functools.partial(pick_kernel, shards), grid=(1,), in_spec...]
  transfers between devices with their start and end apart: 7 -> 8, of which waited for: 6 -> 6; matrix products, arithmetic and copies ran while one was open for 3% -> 2% of each run, Pallas kernels for 9% -> 10%
where the time goes in v5:
time: 123 us
  starting transfers between devices  37 us (30%)
  waiting for transfers between devices  34.9 us (28%)
  Pallas kernels  25.9 us (21%)
  blocking collectives  19.1 us (16%)
  local copies, waits for them, and re-layouts  3.98 us (3%)
    all_to_all x4, starting transfers between devices, exchange(): return lax.all_to_all(array, 'seq', split_axis=0, concat_axis=0, tiled=True)  24.4 us
    pallas_call x2, Pallas kernels, attention_grads(): pl.pallas_call(functools.partial(kernel, per_device, shards, h), grid=(pe...  22.5 us
    all_to_all x1, blocking collectives, exchange(): return lax.all_to_all(array, 'seq', split_axis=0, concat_axis=0, tiled=True)  19.1 us
    ppermute x4, waiting for transfers between devices, shifted(): return lax.ppermute(array, 'seq', pairs)  18.3 us
    all_to_all x4, waiting for transfers between devices, exchange(): return lax.all_to_all(array, 'seq', split_axis=0, concat_axis=0, tiled=True)  16.6 us
    ppermute x4, starting transfers between devices, shifted(): return lax.ppermute(array, 'seq', pairs)  12.6 us
    unnamed x14, local copies, waits for them, and re-layouts  3.69 us
  transfers between devices with their start and end apart: 8, of which 6 were waited for; matrix products, arithmetic and copies ran while one was open for 2% of the time, Pallas kernels for 10%

profile of v5, /device:TPU:10, one launch (start us, length us, event | category | flops | bytes accessed | tf_op | source)
XLA Modules:
  0.0 122.6 jit_solution(1351141461726949211)
XLA Ops:
  0.6 1.4 %wants.1 = s32[8,8,128]{2,1,0:T(8,128)} custom-call(s32[3,4]{1,0:T(4,128)} %ret_ref.5), custom_call_target="tpu_custom_call" | custom-call | tf_op jit(solution)/shard_map/wants/pallas_call | solution.py:215
  2.0 6.2 %all-to-all-start = ((s32[8,8,128]{2,1,0:T(8,128)}), s32[8,8,128]{2,1,0:T(8,128)S(1)}, u32[]{:S(2)}, u32[]{:S(2)}) async-start(s32[8,8,128]{2,1,0:T(8,128)} %wants.1), calls=%async_computation | async-start | bytes 65536 | tf_op jit(solution)/shard_map/all_to_all | solution.py:242
  8.2 1.0 copy.19
  9.2 1.0 copy.20
  10.2 2.4 %all-to-all-done.wants_ref = s32[8,8,128]{2,1,0:T(8,128)S(1)} async-done(((s32[8,8,128]{2,1,0:T(8,128)}), s32[8,8,128]{2,1,0:T(8,128)S(1)}, u32[]{:S(2)}, u32[]{:S(2)}) %all-to-all-start) | async-done | bytes 32800 | tf_op jit(solution)/shard_map/all_to_all | solution.py:242
  12.6 1.0 shard_map.86
  13.6 5.7 %all-to-all-start.2 = ((bf16[8,2,128,128]{3,2,1,0:T(8,128)(2,1)}), bf16[8,2,128,128]{3,2,1,0:T(8,128)(2,1)S(1)}, u32[]{:S(2)}, u32[]{:S(2)}) async-start(bf16[8,2,128,128]{3,2,1,0:T(8,128)(2,1)} %shard_map.86), calls=%async_computation.2 | async-start | bytes 1048576 | tf_op jit(solution)/shard_map/all_to_all | solution.py:242
  19.4 1.0 shard_map.85
  20.4 9.5 %all-to-all-done.2.far_ref = bf16[8,2,128,128]{3,2,1,0:T(8,128)(2,1)S(1)} async-done(((bf16[8,2,128,128]{3,2,1,0:T(8,128)(2,1)}), bf16[8,2,128,128]{3,2,1,0:T(8,128)(2,1)S(1)}, u32[]{:S(2)}, u32[]{:S(2)}) %all-to-all-start.2) | async-done | bytes 524320 | tf_op jit(solution)/shard_map/all_to_all | solution.py:242
  29.9 6.5 %all-to-all-start.1 = ((bf16[8,2,128,128]{3,2,1,0:T(8,128)(2,1)}), bf16[8,2,128,128]{3,2,1,0:T(8,128)(2,1)S(1)}, u32[]{:S(2)}, u32[]{:S(2)}) async-start(bf16[8,2,128,128]{3,2,1,0:T(8,128)(2,1)} %shard_map.85), calls=%async_computation.1 | async-start | bytes 1048576 | tf_op jit(solution)/shard_map/all_to_all | solution.py:242
  36.4 3.4 %collective-permute-start.1 = (bf16[3,2,128,128]{3,2,1,0:T(8,128)(2,1)S(1)}, bf16[3,2,128,128]{3,2,1,0:T(8,128)(2,1)S(1)}, u32[]{:S(2)}, u32[]{:S(2)}) collective-permute-start(bf16[3,2,128,128]{3,2,1,0:T(8,128)(2,1)S(1)} %get-tuple-element.29), channel_id=1, source_target_pairs={{0,1},{1,2},{2,3},{3,4},{4,5},{5,6},{6,7},{8,9},{9,10},{10,11},{11... | collective-permute-start | bytes 589832 | tf_op jit(solution)/shard_map/ppermute | solution.py:248
  39.8 3.4 %collective-permute-start = (bf16[3,2,128,128]{3,2,1,0:T(8,128)(2,1)S(1)}, bf16[3,2,128,128]{3,2,1,0:T(8,128)(2,1)S(1)}, u32[]{:S(2)}, u32[]{:S(2)}) collective-permute-start(bf16[3,2,128,128]{3,2,1,0:T(8,128)(2,1)S(1)} %get-tuple-element.30), channel_id=1, source_target_pairs={{0,1},{1,2},{2,3},{3,4},{4,5},{5,6},{6,7},{8,9},{9,10},{10,11},{11... | collective-permute-start | bytes 589832 | tf_op jit(solution)/shard_map/ppermute | solution.py:248
  43.2 8.5 %collective-permute-done.1.prev_ref = bf16[3,2,128,128]{3,2,1,0:T(8,128)(2,1)S(1)} collective-permute-done((bf16[3,2,128,128]{3,2,1,0:T(8,128)(2,1)S(1)}, bf16[3,2,128,128]{3,2,1,0:T(8,128)(2,1)S(1)}, u32[]{:S(2)}, u32[]{:S(2)}) %collective-permute-start.1) | collective-permute-done | bytes 196640 | tf_op jit(solution)/shard_map/ppermute | solution.py:248
  51.7 11.2 %shard_map.87 = (bf16[14,384,128]{2,1,0:T(8,128)(2,1)}, f32[2,3,2,128,128]{4,3,2,1,0:T(8,128)}, bf16[3,2,128,128]{3,2,1,0:T(8,128)(2,1)}, bf16[8,2,128,128]{3,2,1,0:T(8,128)(2,1)}) custom-call(s32[1]{0:T(128)} %bitcast.own_ref, s32[3]{0:T(128)S(1)} %copy-done.1, s32[3,4]{1,0:T(4,128)S(1)} %copy-done, bf16[14,384,128]{2,1,0:T(8,128)(2,1)} %bitcast.46, ...), custom_call_target="tpu_custom_call" | custom-call | flops 3523215360 | bytes 5505024 | tf_op jit(solution)/shard_map/pallas_call | solution.py:174
  62.9 11.2 %shard_map.88 = (bf16[14,384,128]{2,1,0:T(8,128)(2,1)}, f32[2,3,2,128,128]{4,3,2,1,0:T(8,128)}, bf16[3,2,128,128]{3,2,1,0:T(8,128)(2,1)}, bf16[8,2,128,128]{3,2,1,0:T(8,128)(2,1)}) custom-call(s32[1]{0:T(128)} %bitcast.own_ref, s32[3]{0:T(128)S(1)} %copy-done.1, s32[3,4]{1,0:T(4,128)S(1)} %copy-done, ...), custom_call_target="tpu_custom_call", output_to_operand_aliasing={{0}: (8, {}), {1}: (9, {})} | custom-call | flops 3523215360 | bytes 5505024 | tf_op jit(solution)/shard_map/pallas_call | solution.py:174
  74.2 19.1 %all_to_all.25 = bf16[8,2,128,128]{3,2,1,0:T(8,128)(2,1)S(1)} all-to-all(bf16[8,2,128,128]{3,2,1,0:T(8,128)(2,1)} %get-tuple-element.18), channel_id=1, replica_groups=mesh['dp'=4,'seq'=8] {'seq'}, dimensions={0} | all-to-all | bytes 1048576 | tf_op jit(solution)/shard_map/all_to_all | solution.py:242
  93.3 5.9 %all-to-all-start.3 = ((bf16[8,2,128,128]{3,2,1,0:T(8,128)(2,1)}), bf16[8,2,128,128]{3,2,1,0:T(8,128)(2,1)S(1)}, u32[]{:S(2)}, u32[]{:S(2)}) async-start(bf16[8,2,128,128]{3,2,1,0:T(8,128)(2,1)} %get-tuple-element.16), calls=%async_computation.3 | async-start | bytes 1048576 | tf_op jit(solution)/shard_map/all_to_all | solution.py:242
  99.5 2.5 %collective-permute-start.3 = (bf16[3,2,128,128]{3,2,1,0:T(8,128)(2,1)S(1)}, bf16[3,2,128,128]{3,2,1,0:T(8,128)(2,1)S(1)}, u32[]{:S(2)}, u32[]{:S(2)}) collective-permute-start(bf16[3,2,128,128]{3,2,1,0:T(8,128)(2,1)S(1)} %copy-done.4), channel_id=1, source_target_pairs={{1,0},{2,1},{3,2},{4,3},{5,4},{6,5},{7,6},{9,8},{10,9},{11,10},{12... | collective-permute-start | bytes 589832 | tf_op jit(solution)/shard_map/ppermute | solution.py:248
  102.0 3.4 %collective-permute-start.2 = (bf16[3,2,128,128]{3,2,1,0:T(8,128)(2,1)S(1)}, bf16[3,2,128,128]{3,2,1,0:T(8,128)(2,1)S(1)}, u32[]{:S(2)}, u32[]{:S(2)}) collective-permute-start(bf16[3,2,128,128]{3,2,1,0:T(8,128)(2,1)S(1)} %copy-done.3), channel_id=1, source_target_pairs={{1,0},{2,1},{3,2},{4,3},{5,4},{6,5},{7,6},{9,8},{10,9},{11,10},{12... | collective-permute-start | bytes 589832 | tf_op jit(solution)/shard_map/ppermute | solution.py:248
  105.8 4.7 %all-to-all-done.3 = bf16[8,2,128,128]{3,2,1,0:T(8,128)(2,1)S(1)} async-done(((bf16[8,2,128,128]{3,2,1,0:T(8,128)(2,1)}), bf16[8,2,128,128]{3,2,1,0:T(8,128)(2,1)S(1)}, u32[]{:S(2)}, u32[]{:S(2)}) %all-to-all-start.3) | async-done | bytes 524320 | tf_op jit(solution)/shard_map/all_to_all | solution.py:242
  110.9 7.0 %collective-permute-done.3 = bf16[3,2,128,128]{3,2,1,0:T(8,128)(2,1)S(1)} collective-permute-done((bf16[3,2,128,128]{3,2,1,0:T(8,128)(2,1)S(1)}, bf16[3,2,128,128]{3,2,1,0:T(8,128)(2,1)S(1)}, u32[]{:S(2)}, u32[]{:S(2)}) %collective-permute-start.3) | collective-permute-done | bytes 196640 | tf_op jit(solution)/shard_map/ppermute | solution.py:248
  117.9 2.8 %collective-permute-done.2 = bf16[3,2,128,128]{3,2,1,0:T(8,128)(2,1)S(1)} collective-permute-done((bf16[3,2,128,128]{3,2,1,0:T(8,128)(2,1)S(1)}, bf16[3,2,128,128]{3,2,1,0:T(8,128)(2,1)S(1)}, u32[]{:S(2)}, u32[]{:S(2)}) %collective-permute-start.2) | collective-permute-done | bytes 196640 | tf_op jit(solution)/shard_map/ppermute | solution.py:248
  120.9 0.9 copy.26
  121.8 0.9 copy.25
  (20 shorter events, 1.3 us)
Async XLA Ops:
  2.0 10.6 %all-to-all-start = ((s32[8,8,128]{2,1,0:T(8,128)}), s32[8,8,128]{2,1,0:T(8,128)S(1)}, u32[]{:S(2)}, u32[]{:S(2)}) async-start(s32[8,8,128]{2,1,0:T(8,128)} %wants.1), calls=%async_computation | async-start | bytes 65536 | tf_op jit(solution)/shard_map/all_to_all | solution.py:242
  13.6 16.2 %all-to-all-start.2 = ((bf16[8,2,128,128]{3,2,1,0:T(8,128)(2,1)}), bf16[8,2,128,128]{3,2,1,0:T(8,128)(2,1)S(1)}, u32[]{:S(2)}, u32[]{:S(2)}) async-start(bf16[8,2,128,128]{3,2,1,0:T(8,128)(2,1)} %shard_map.86), calls=%async_computation.2 | async-start | bytes 1048576 | tf_op jit(solution)/shard_map/all_to_all | solution.py:242
  19.4 32.3 %copy-start = (s32[3,4]{1,0:T(4,128)S(1)}, s32[3,4]{1,0:T(4,128)}, u32[]{:S(2)}) copy-start(s32[3,4]{1,0:T(4,128)} %ret_ref.5) | copy-start | bytes 148
  19.4 32.3 %copy-start.1 = (s32[3]{0:T(128)S(1)}, s32[3]{0:T(128)}, u32[]{:S(2)}) copy-start(s32[3]{0:T(128)} %win_ref.3) | copy-start | bytes 40
  29.9 33.1 %all-to-all-start.1 = ((bf16[8,2,128,128]{3,2,1,0:T(8,128)(2,1)}), bf16[8,2,128,128]{3,2,1,0:T(8,128)(2,1)S(1)}, u32[]{:S(2)}, u32[]{:S(2)}) async-start(bf16[8,2,128,128]{3,2,1,0:T(8,128)(2,1)} %shard_map.85), calls=%async_computation.1 | async-start | bytes 1048576 | tf_op jit(solution)/shard_map/all_to_all | solution.py:242
  36.4 15.3 %collective-permute-start.1 = (bf16[3,2,128,128]{3,2,1,0:T(8,128)(2,1)S(1)}, bf16[3,2,128,128]{3,2,1,0:T(8,128)(2,1)S(1)}, u32[]{:S(2)}, u32[]{:S(2)}) collective-permute-start(bf16[3,2,128,128]{3,2,1,0:T(8,128)(2,1)S(1)} %get-tuple-element.29), channel_id=1, source_target_pairs={{0,1},{1,2},{2,3},{3,4},{4,5},{5,6},{6,7},{8,9},{9,10},{10,11},{11... | collective-permute-start | bytes 589832 | tf_op jit(solution)/shard_map/ppermute | solution.py:248
  39.8 23.2 %collective-permute-start = (bf16[3,2,128,128]{3,2,1,0:T(8,128)(2,1)S(1)}, bf16[3,2,128,128]{3,2,1,0:T(8,128)(2,1)S(1)}, u32[]{:S(2)}, u32[]{:S(2)}) collective-permute-start(bf16[3,2,128,128]{3,2,1,0:T(8,128)(2,1)S(1)} %get-tuple-element.30), channel_id=1, source_target_pairs={{0,1},{1,2},{2,3},{3,4},{4,5},{5,6},{6,7},{8,9},{9,10},{10,11},{11... | collective-permute-start | bytes 589832 | tf_op jit(solution)/shard_map/ppermute | solution.py:248
  74.2 25.3 %copy-start.4 = (bf16[3,2,128,128]{3,2,1,0:T(8,128)(2,1)S(1)}, bf16[3,2,128,128]{3,2,1,0:T(8,128)(2,1)}, u32[]{:S(2)}) copy-start(bf16[3,2,128,128]{3,2,1,0:T(8,128)(2,1)} %get-tuple-element.17) | copy-start | bytes 589828
  74.2 27.8 %copy-start.3 = (bf16[3,2,128,128]{3,2,1,0:T(8,128)(2,1)S(1)}, bf16[3,2,128,128]{3,2,1,0:T(8,128)(2,1)}, u32[]{:S(2)}) copy-start(bf16[3,2,128,128]{3,2,1,0:T(8,128)(2,1)} %get-tuple-element.15) | copy-start | bytes 589828
  93.3 27.4 %copy-start.2 = (f32[2,3,2,128,128]{4,3,2,1,0:T(8,128)S(1)}, f32[2,3,2,128,128]{4,3,2,1,0:T(8,128)}, u32[]{:S(2)}) copy-start(f32[2,3,2,128,128]{4,3,2,1,0:T(8,128)} %get-tuple-element.14) | copy-start | bytes 2359300
  93.3 17.2 %all-to-all-start.3 = ((bf16[8,2,128,128]{3,2,1,0:T(8,128)(2,1)}), bf16[8,2,128,128]{3,2,1,0:T(8,128)(2,1)S(1)}, u32[]{:S(2)}, u32[]{:S(2)}) async-start(bf16[8,2,128,128]{3,2,1,0:T(8,128)(2,1)} %get-tuple-element.16), calls=%async_computation.3 | async-start | bytes 1048576 | tf_op jit(solution)/shard_map/all_to_all | solution.py:242
  99.5 18.4 %collective-permute-start.3 = (bf16[3,2,128,128]{3,2,1,0:T(8,128)(2,1)S(1)}, bf16[3,2,128,128]{3,2,1,0:T(8,128)(2,1)S(1)}, u32[]{:S(2)}, u32[]{:S(2)}) collective-permute-start(bf16[3,2,128,128]{3,2,1,0:T(8,128)(2,1)S(1)} %copy-done.4), channel_id=1, source_target_pairs={{1,0},{2,1},{3,2},{4,3},{5,4},{6,5},{7,6},{9,8},{10,9},{11,10},{12... | collective-permute-start | bytes 589832 | tf_op jit(solution)/shard_map/ppermute | solution.py:248
  102.0 18.7 %collective-permute-start.2 = (bf16[3,2,128,128]{3,2,1,0:T(8,128)(2,1)S(1)}, bf16[3,2,128,128]{3,2,1,0:T(8,128)(2,1)S(1)}, u32[]{:S(2)}, u32[]{:S(2)}) collective-permute-start(bf16[3,2,128,128]{3,2,1,0:T(8,128)(2,1)S(1)} %copy-done.3), channel_id=1, source_target_pairs={{1,0},{2,1},{3,2},{4,3},{5,4},{6,5},{7,6},{9,8},{10,9},{11,10},{12... | collective-permute-start | bytes 589832 | tf_op jit(solution)/shard_map/ppermute | solution.py:248
